TPU v7x, 32 devices: a whole 2x2x4 slice. The times are simulated.
32 devices in a mesh: dp: 8 (over z, x), tensor: 4 (over y, core).
Axes of the slice: x: 2, y: 2, z: 4, core: 2. Of those that a mesh axis runs over, the one named last changes fastest.
Arguments:
- hidden_in: bfloat16 [1024, 32, 768], P('tensor', 'dp'), may hold values from -6 to 6
- cotangent: bfloat16 [1024, 32, 768], P('tensor', 'dp'), may hold values from -6 to 6
- prefix: int32 [32], P('dp'), may hold values from 102 to 512, as said below
- w_qkv: bfloat16 [768, 3, 768], P('dp', None, 'tensor'), may hold values from -0.21875 to 0.21875
- w_out: bfloat16 [768, 768], P('tensor', 'dp'), may hold values from -3 to 3
- w_in: bfloat16 [768, 3072], P('dp', 'tensor'), may hold values from -0.21875 to 0.21875
- w_down: bfloat16 [3072, 768], P('tensor', 'dp'), may hold values from -0.109375 to 0.109375
- biases: float32 [10, 768], P(None, ('dp', 'tensor')), may hold values from -1 to 1
- gains: float32 [2, 768], P(None, ('dp', 'tensor')), may hold values from 0.25 to 1.75
Outputs:
- output: bfloat16 [1024, 32, 768], P('tensor', 'dp')
- grad_input: bfloat16 [1024, 32, 768], P('tensor', 'dp')
- grad_qkv: float32 [768, 3, 768], P('dp', None, 'tensor')
- grad_out: float32 [768, 768], P('tensor', 'dp')
- grad_in: float32 [768, 3072], P('dp', 'tensor')
- grad_down: float32 [3072, 768], P('tensor', 'dp')
- grad_biases: float32 [10, 768], P(None, ('dp', 'tensor'))
- grad_gains: float32 [2, 768], P(None, ('dp', 'tensor'))
Inputs may be any that keep to these rules, and one draw needn't show every extreme that they name: Every draw has a sequence whose prefix is 512.
All inputs are finite; a program needn't handle non-finite values.
Results may differ from a plain program's by a relative error of at most 0.018.
Values may be sent and summed in bfloat16 or wider, within the bound.
A program may use at most 192 MiB of HBM per device.

v0:
```python
import math

import jax
import jax.numpy as jnp
from jax import lax
from jax.sharding import PartitionSpec as P

HEAD = 64
FF = 3072
SEQ_MICRO = 2


EPSILON = 1e-12
MASKED = -1e30


def in_blocks(array, dim, devices):
    before, after = (array.shape[:dim], array.shape[dim + 1 :])
    return jnp.moveaxis(array.reshape(*before, devices, -1, *after), dim, 0)


def sent_and_summed(array, axis, dim):
    blocks = in_blocks(array, dim, lax.axis_size(axis))
    arrived = lax.all_to_all(blocks, axis, split_axis=0, concat_axis=0, tiled=True)
    return arrived.astype(jnp.float32).sum(axis=0)


def side_by_side(arrays, axis, dim, along):
    widths = [math.prod(a.shape[along:]) for a in arrays]
    both = jnp.concatenate(
        [a.reshape(*a.shape[:along], w) for a, w in zip(arrays, widths)], axis=along
    )
    filled = sent_and_summed(both, axis, dim)
    blocks = jnp.split(filled, [sum(widths[:k]) for k in range(1, len(widths))], axis=along)
    return tuple(
        (b.reshape(*filled.shape[:along], *a.shape[along:]) for a, b in zip(arrays, blocks))
    )


def side_by_side_2(arrays, axis, dim, along):
    both = jnp.concatenate(arrays, axis=along)
    filled, at, gathered = (sent_and_summed(both, axis, dim), 0, [])
    for a in arrays:
        gathered.append(lax.slice_in_dim(filled, at, at + a.shape[along], axis=along))
        at += a.shape[along]
    return tuple(gathered)


def layer_norm(inputs, gain_vec, offset):
    center = inputs - jnp.mean(inputs, axis=-1, keepdims=True)
    spread = jnp.mean(center * center, axis=-1, keepdims=True)
    return center * lax.rsqrt(spread + EPSILON) * gain_vec + offset


def gelu_exact(inputs):
    return jax.nn.gelu(inputs, approximate=False)


def visible(prefix_here, first_row, block_rows, key_total):
    query_pos = first_row + jnp.arange(block_rows, dtype=jnp.int32)
    key_pos = jnp.arange(key_total, dtype=jnp.int32)
    causal = key_pos[None, :] <= query_pos[:, None]
    opened = key_pos[None, None, :] < prefix_here[:, None, None]
    return jnp.logical_or(causal[None], opened)[:, None]


def attend(queries, keys_all, values_all, prefix_here, block_rows, score_scale):
    length = queries.shape[0]
    out_blocks = []
    lse_blocks = []
    for block_index in range(length // block_rows):
        first_row = block_index * block_rows
        query_block = queries[first_row : first_row + block_rows]
        scores = (
            jnp.einsum("qshd,kshd->shqk", query_block, keys_all, preferred_element_type=jnp.float32)
            * score_scale
        )
        scores = jnp.where(visible(prefix_here, first_row, block_rows, length), scores, MASKED)
        row_peak = jnp.max(scores, axis=-1, keepdims=True)
        weights = jnp.exp(scores - row_peak)
        row_total = jnp.sum(weights, axis=-1, keepdims=True)
        probs_low = (weights / row_total).astype(jnp.bfloat16)
        mixed = jnp.einsum(
            "shqk,kshd->qshd", probs_low, values_all, preferred_element_type=jnp.float32
        )
        out_blocks.append(mixed.astype(jnp.bfloat16))
        lse_blocks.append(row_peak + jnp.log(row_total))
    return (jnp.concatenate(out_blocks, 0), jnp.concatenate(lse_blocks, 2))


def attend_back(
    queries, keys_all, values_all, grad_heads, log_sums, prefix_here, block_rows, score_scale
):
    length = queries.shape[0]
    grad_query = []
    grad_keys = jnp.zeros(keys_all.shape, jnp.float32)
    grad_values = jnp.zeros(values_all.shape, jnp.float32)
    for block_index in range(length // block_rows):
        first_row = block_index * block_rows
        query_block = queries[first_row : first_row + block_rows]
        grad_block = grad_heads[first_row : first_row + block_rows]
        scores = (
            jnp.einsum("qshd,kshd->shqk", query_block, keys_all, preferred_element_type=jnp.float32)
            * score_scale
        )
        scores = jnp.where(visible(prefix_here, first_row, block_rows, length), scores, MASKED)
        probs = jnp.exp(scores - log_sums[:, :, first_row : first_row + block_rows])
        probs_low = probs.astype(jnp.bfloat16)
        grad_probs = jnp.einsum(
            "qshd,kshd->shqk", grad_block, values_all, preferred_element_type=jnp.float32
        )
        grad_scores = probs * (grad_probs - jnp.sum(probs * grad_probs, axis=-1, keepdims=True))
        scores_low = (grad_scores * score_scale).astype(jnp.bfloat16)
        grad_query.append(
            jnp.einsum("shqk,kshd->qshd", scores_low, keys_all, preferred_element_type=jnp.float32)
        )
        padding = ((0, length - length), (0, 0), (0, 0), (0, 0))
        grad_keys = grad_keys + jnp.pad(
            jnp.einsum(
                "shqk,qshd->kshd", scores_low, query_block, preferred_element_type=jnp.float32
            ),
            padding,
        )
        grad_values = grad_values + jnp.pad(
            jnp.einsum(
                "shqk,qshd->kshd", probs_low, grad_block, preferred_element_type=jnp.float32
            ),
            padding,
        )
    return (jnp.concatenate(grad_query, 0), grad_keys, grad_values)


def place_slice(vector, total_len, tensor_index):
    return lax.dynamic_update_slice_in_dim(
        jnp.zeros((total_len,), jnp.float32), vector, tensor_index * vector.shape[0], 0
    )


def fetch_weights(w_qkv, w_in, w_out, w_down):
    row_mats = (
        lax.all_gather(w_qkv, "dp", axis=0, tiled=True),
        lax.all_gather(w_in, "dp", axis=0, tiled=True),
    )
    col_mats = (
        lax.all_gather(w_out, "dp", axis=1, tiled=True),
        lax.all_gather(w_down, "dp", axis=1, tiled=True),
    )
    return (row_mats[0], row_mats[1], col_mats[0], col_mats[1])


def reduce_weights(grad_terms):
    row_sums = side_by_side(
        (grad_terms[0].astype(jnp.bfloat16), grad_terms[1].astype(jnp.bfloat16)), "dp", 0, 1
    )
    col_sums = side_by_side_2(
        (grad_terms[2].astype(jnp.bfloat16), grad_terms[3].astype(jnp.bfloat16)), "dp", 1, 0
    )
    return (row_sums[0], row_sums[1], col_sums[0], col_sums[1])


def micro_step(hidden_m, cot_m, prefix_m, weights, vectors, tensor_index):
    mat_qkv, mat_in, mat_out, mat_down = weights
    bias_q, bias_v, bias_out, bias_hidden, bias_down, shift_one, shift_two, gain_one, gain_two = (
        vectors
    )
    rows_here, seq_count, model_width = hidden_m.shape
    local_width = mat_qkv.shape[2]
    heads_here = local_width // HEAD
    score_scale = HEAD ** (-0.5)
    gathered = lax.all_gather(hidden_m, "tensor", axis=0, tiled=True)
    length = gathered.shape[0]
    block_rows = length // 2
    bias_three = jnp.stack([bias_q, jnp.zeros_like(bias_q), bias_v])
    proj_qkv = (
        jnp.einsum("psd,dch->psch", gathered, mat_qkv, preferred_element_type=jnp.float32)
        + bias_three
    ).astype(jnp.bfloat16)
    qkv_heads = proj_qkv.reshape(length, seq_count, 3, heads_here, HEAD)
    queries, keys_all, values_all = (qkv_heads[:, :, 0], qkv_heads[:, :, 1], qkv_heads[:, :, 2])
    heads_out, log_sums = attend(queries, keys_all, values_all, prefix_m, block_rows, score_scale)
    heads_flat = heads_out.reshape(length, seq_count, local_width)
    row_block = heads_flat
    attn_branch = lax.psum_scatter(
        jnp.einsum("psh,hd->psd", row_block, mat_out, preferred_element_type=jnp.float32).astype(
            jnp.bfloat16
        ),
        "tensor",
        scatter_dimension=0,
        tiled=True,
    ).astype(jnp.float32)
    resid_one = hidden_m.astype(jnp.float32) + attn_branch + bias_out
    normed, norm_one_back = jax.vjp(layer_norm, resid_one, gain_one, shift_one)
    normed_all = lax.all_gather(normed.astype(jnp.bfloat16), "tensor", axis=0, tiled=True)
    pre_act = (
        jnp.einsum("psd,df->psf", normed_all, mat_in, preferred_element_type=jnp.float32)
        + bias_hidden
    )
    act_value, gelu_back = jax.vjp(gelu_exact, pre_act)
    activated = act_value.astype(jnp.bfloat16)
    row_block = activated
    ffn_branch = lax.psum_scatter(
        jnp.einsum("psf,fd->psd", row_block, mat_down, preferred_element_type=jnp.float32).astype(
            jnp.bfloat16
        ),
        "tensor",
        scatter_dimension=0,
        tiled=True,
    ).astype(jnp.float32)
    resid_two = normed + ffn_branch + bias_down
    out_value, norm_two_back = jax.vjp(layer_norm, resid_two, gain_two, shift_two)
    grad_two, grad_gain_two, grad_shift_two = norm_two_back(cot_m.astype(jnp.float32))
    grad_bias_down = jnp.sum(grad_two, axis=(0, 1))
    grad_two_all = lax.all_gather(grad_two.astype(jnp.bfloat16), "tensor", axis=0, tiled=True)
    grad_down = jnp.einsum(
        "psf,psd->fd", activated, grad_two_all, preferred_element_type=jnp.float32
    )
    grad_act = jnp.einsum("psd,fd->psf", grad_two_all, mat_down, preferred_element_type=jnp.float32)
    grad_pre = gelu_back(grad_act)[0].astype(jnp.bfloat16)
    grad_in = jnp.einsum("psd,psf->df", normed_all, grad_pre, preferred_element_type=jnp.float32)
    grad_bias_hidden = jnp.sum(grad_pre, axis=(0, 1), dtype=jnp.float32)
    row_block = grad_pre
    grad_normed = grad_two + lax.psum_scatter(
        jnp.einsum("psf,df->psd", row_block, mat_in, preferred_element_type=jnp.float32).astype(
            jnp.bfloat16
        ),
        "tensor",
        scatter_dimension=0,
        tiled=True,
    ).astype(jnp.float32)
    grad_one, grad_gain_one, grad_shift_one = norm_one_back(grad_normed)
    grad_bias_out = jnp.sum(grad_one, axis=(0, 1))
    grad_one_all = lax.all_gather(grad_one.astype(jnp.bfloat16), "tensor", axis=0, tiled=True)
    grad_out = jnp.einsum(
        "psh,psd->hd", heads_flat, grad_one_all, preferred_element_type=jnp.float32
    )
    grad_heads = jnp.einsum(
        "psd,hd->psh", grad_one_all, mat_out, preferred_element_type=jnp.float32
    ).astype(jnp.bfloat16)
    grad_heads = grad_heads.reshape(length, seq_count, heads_here, HEAD)
    grad_query, grad_keys, grad_values = attend_back(
        queries, keys_all, values_all, grad_heads, log_sums, prefix_m, block_rows, score_scale
    )
    grad_proj = (
        jnp.stack([grad_query, grad_keys, grad_values], axis=2)
        .astype(jnp.bfloat16)
        .reshape(length, seq_count, 3, local_width)
    )
    grad_qkv = jnp.einsum("psd,psch->dch", gathered, grad_proj, preferred_element_type=jnp.float32)
    grad_bias_q = jnp.sum(grad_proj[:, :, 0], axis=(0, 1), dtype=jnp.float32)
    grad_bias_v = jnp.sum(grad_proj[:, :, 2], axis=(0, 1), dtype=jnp.float32)
    row_block = grad_proj
    grad_hidden = grad_one + lax.psum_scatter(
        jnp.einsum("psch,dch->psd", row_block, mat_qkv, preferred_element_type=jnp.float32).astype(
            jnp.bfloat16
        ),
        "tensor",
        scatter_dimension=0,
        tiled=True,
    ).astype(jnp.float32)
    hidden_rows = place_slice(grad_bias_hidden, FF, tensor_index).reshape(
        FF // model_width, model_width
    )
    bias_grad = jnp.concatenate(
        [
            place_slice(grad_bias_q, model_width, tensor_index)[None],
            place_slice(grad_bias_v, model_width, tensor_index)[None],
            grad_bias_out[None],
            hidden_rows,
            grad_bias_down[None],
            grad_shift_one[None],
            grad_shift_two[None],
        ],
        axis=0,
    )
    gain_grad = jnp.stack([grad_gain_one, grad_gain_two])
    return (
        out_value.astype(jnp.bfloat16),
        grad_hidden.astype(jnp.bfloat16),
        (grad_qkv, grad_in, grad_out, grad_down),
        (bias_grad, gain_grad),
    )


def on_device(hidden_in, cotangent, prefix, w_qkv, w_out, w_in, w_down, biases, gains):
    biases_all, gains_all = (
        lax.all_gather(biases, ("dp", "tensor"), axis=1, tiled=True),
        lax.all_gather(gains, ("dp", "tensor"), axis=1, tiled=True),
    )
    tensor_index = lax.axis_index("tensor")
    model_width = biases_all.shape[1]
    local_width = w_qkv.shape[2]
    hidden_here = w_in.shape[1]
    rows_hidden = FF // model_width
    vectors = (
        lax.dynamic_slice_in_dim(biases_all[0], tensor_index * local_width, local_width, 0),
        lax.dynamic_slice_in_dim(biases_all[1], tensor_index * local_width, local_width, 0),
        biases_all[2],
        lax.dynamic_slice_in_dim(
            biases_all[3 : 3 + rows_hidden].reshape(FF), tensor_index * hidden_here, hidden_here, 0
        ),
        biases_all[3 + rows_hidden],
        biases_all[4 + rows_hidden],
        biases_all[5 + rows_hidden],
        gains_all[0],
        gains_all[1],
    )
    n_micro = hidden_in.shape[1] // SEQ_MICRO

    def take_micro(source, micro_index):
        return lax.dynamic_slice_in_dim(source, micro_index * SEQ_MICRO, SEQ_MICRO, 1)

    def run_micro(micro_index, weights):
        prefix_m = lax.dynamic_slice_in_dim(prefix, micro_index * SEQ_MICRO, SEQ_MICRO, 0)
        return micro_step(
            take_micro(hidden_in, micro_index),
            take_micro(cotangent, micro_index),
            prefix_m,
            weights,
            vectors,
            tensor_index,
        )

    def store_micro(buffer, new_piece, micro_index):
        return lax.dynamic_update_slice_in_dim(buffer, new_piece, micro_index * SEQ_MICRO, 1)

    small_start = (
        jnp.zeros(biases_all.shape, jnp.float32),
        jnp.zeros(gains_all.shape, jnp.float32),
    )
    out_start = jnp.zeros_like(hidden_in)
    grad_start = jnp.zeros_like(hidden_in)
    shard_start = (
        jnp.zeros(w_qkv.shape, jnp.float32),
        jnp.zeros(w_in.shape, jnp.float32),
        jnp.zeros(w_out.shape, jnp.float32),
        jnp.zeros(w_down.shape, jnp.float32),
    )

    def micro_loop(micro_index, loop_state):
        out_buf, grad_buf, shard_sum, small_sum = loop_state
        out_m, grad_m, grad_terms, small_terms = run_micro(
            micro_index, fetch_weights(w_qkv, w_in, w_out, w_down)
        )
        shards = reduce_weights(grad_terms)
        return (
            store_micro(out_buf, out_m, micro_index),
            store_micro(grad_buf, grad_m, micro_index),
            tuple((acc + term for acc, term in zip(shard_sum, shards))),
            tuple((acc + term for acc, term in zip(small_sum, small_terms))),
        )

    out_buf, grad_buf, shard_sum, small_sum = lax.fori_loop(
        0, n_micro, micro_loop, (out_start, grad_start, shard_start, small_start)
    )
    grad_bias_shard, grad_gain_shard = (
        lax.psum_scatter(small_sum[0], ("dp", "tensor"), scatter_dimension=1, tiled=True),
        lax.psum_scatter(small_sum[1], ("dp", "tensor"), scatter_dimension=1, tiled=True),
    )
    return (
        out_buf,
        grad_buf,
        shard_sum[0],
        shard_sum[2],
        shard_sum[1],
        shard_sum[3],
        grad_bias_shard,
        grad_gain_shard,
    )


def solution(mesh):
    placed = (
        P("tensor", "dp", None),
        P("tensor", "dp", None),
        P("dp"),
        P("dp", None, "tensor"),
        P("tensor", "dp"),
        P("dp", "tensor"),
        P("tensor", "dp"),
        P(None, ("dp", "tensor")),
        P(None, ("dp", "tensor")),
    )
    return jax.shard_map(
        on_device,
        mesh=mesh,
        in_specs=placed,
        out_specs=(
            P("tensor", "dp", None),
            P("tensor", "dp", None),
            P("dp", None, "tensor"),
            P("tensor", "dp"),
            P("dp", "tensor"),
            P("tensor", "dp"),
            P(None, ("dp", "tensor")),
            P(None, ("dp", "tensor")),
        ),
        check_vma=False,
    )
```

profile of v0, /device:TPU:0, one launch (start us, length us, event | category | flops | bytes accessed | tf_op | source)
XLA Modules:
  0.0 1480.5 jit_solution(16612844014903660465)
XLA Ops:
  7.2 43.6 %all-gather.1 = f32[32,24,2]{1,2,0:T(2,128)S(1)} all-gather(f32[1,24,2]{1,2,0:T(2,128)} %bitcast.322), channel_id=1, replica_groups=mesh['dp'=8,'tensor'=4] {'dp','tensor'}, dimensions={0}, use_global_device_ids=true | all-gather | bytes 6336 | tf_op jit(solution)/shard_map/all_gather | solution.py:287
  54.1 37.6 %all-gather = f32[32,24,10]{1,2,0:T(8,128)S(1)} all-gather(f32[1,24,10]{1,2,0:T(8,128)} %bitcast.321), channel_id=1, replica_groups=mesh['dp'=8,'tensor'=4] {'dp','tensor'}, dimensions={0}, use_global_device_ids=true | all-gather | bytes 31680 | tf_op jit(solution)/shard_map/all_gather | solution.py:286
  96.3 1334.1 %while.30 = (s32[]{:T(128)}, bf16[256,4,768]{2,1,0:T(4,128)(2,1)}, bf16[256,4,768]{2,1,0:T(4,128)(2,1)}, f32[96,3,192]{0,2,1:T(8,128)}, f32[96,768]{1,0:T(8,128)...) while((s32[]{:T(128)}, bf16[256,4,768]{2,1,0:T(4,128)(2,1)}, ...), condition=%wide.region_30.0_spmd.clone, body=%wide.region_0.30_spmd.clone.sunk | while | flops 27052142592 | bytes 971276288 | solution.py:352
  100.4 37.0 %all_gather.97 = bf16[768,3,192]{2,1,0:T(4,128)(2,1)S(1)} all-gather(bf16[96,3,192]{2,1,0:T(4,128)(2,1)} %get-tuple-element.1198), channel_id=1, replica_groups=mesh['dp'=8,'tensor'=4] {'dp'}, dimensions={0}, use_global_device_ids=true | all-gather | bytes 995328 | tf_op jit(solution)/shard_map/while/body/eval_jaxpr/all_gather | solution.py:141
  139.8 33.3 %all_gather.98 = bf16[192,768]{0,1:T(8,128)(2,1)} all-gather(bf16[192,96]{0,1:T(8,128)(2,1)} %get-tuple-element.1202), channel_id=1, replica_groups=mesh['dp'=8,'tensor'=4] {'dp'}, dimensions={1}, use_global_device_ids=true | all-gather | bytes 331776 | tf_op jit(solution)/shard_map/while/body/eval_jaxpr/all_gather | solution.py:145
  187.2 7.1 fusion.264
  194.3 5.3 fusion.266
  199.6 5.3 fusion.265
  211.0 35.6 %reduce-scatter.7.cloned.1.call-done = bf16[256,2,768]{2,0,1:T(8,128)(2,1)} async-done(((bf16[1024,2,768]{2,0,1:T(8,128)(2,1)}), bf16[256,2,768]{2,0,1:T(8,128)(2,1)}) %reduce-scatter.7.cloned.1.call-update) | async-done | bytes 786448 | tf_op jit(solution)/shard_map/while/body/eval_jaxpr/reduce_scatter | solution.py:183
  252.8 37.1 %all-gather.13.cloned.1.call-done = bf16[768,768]{1,0:T(8,128)(2,1)} async-done(((bf16[96,768]{1,0:T(8,128)(2,1)}), bf16[768,768]{1,0:T(8,128)(2,1)}) %all-gather.13.cloned.1.call-update) | async-done | bytes 1179664 | tf_op jit(solution)/shard_map/while/body/eval_jaxpr/all_gather | solution.py:142
  289.9 28.7 %all-gather.11.cloned.1.call-done = bf16[1024,2,768]{2,0,1:T(8,128)(2,1)} async-done(((bf16[256,2,768]{2,0,1:T(8,128)(2,1)}), bf16[1024,2,768]{2,0,1:T(8,128)(2,1)}) %all-gather.11.cloned.1.call-update) | async-done | bytes 3145744 | tf_op jit(solution)/shard_map/while/body/eval_jaxpr/all_gather | solution.py:193
  318.6 6.7 fusion.270
  328.0 15.7 %multiply_convert_fusion.4 = (bf16[1024,2,768]{2,0,1:T(8,128)(2,1)}, f32[1024,2,768]{2,0,1:T(8,128)}) fusion(f32[1024,2,768]{2,0,1:T(8,128)S(1)} %get-tuple-element.1095, f32[768]{0:T(1024)S(1)} %get-tuple-element.1207, u8[1024,768]{1,0:T(8,128)(4,1)S(1)} %get-tuple-element.1096, u8[1024,768]{1,0:T(8,128)(4,1)S(1)} %get-tuple-element.1097), kind=kLoop, calls=%fused_computation.40.clone.1 | loop fusion | flops 111673344 | bytes 17304576 | tf_op jit(solution)/shard_map/while/body/eval_jaxpr/convert_element_type | solution.py:199
  343.7 18.1 %all-gather.15.cloned.1.call-done = bf16[768,768]{0,1:T(8,128)(2,1)} async-done(((bf16[768,96]{0,1:T(8,128)(2,1)}), bf16[768,768]{0,1:T(8,128)(2,1)}) %all-gather.15.cloned.1.call-update) | async-done | bytes 1179664 | tf_op jit(solution)/shard_map/while/body/eval_jaxpr/all_gather | solution.py:146
  361.8 6.6 convolution_convert_fusion.9
  371.6 33.5 %reduce-scatter.9.cloned.1.call-done = bf16[256,2,768]{2,0,1:T(8,128)(2,1)} async-done(((bf16[1024,2,768]{2,0,1:T(8,128)(2,1)}), bf16[256,2,768]{2,0,1:T(8,128)(2,1)}) %reduce-scatter.9.cloned.1.call-update) | async-done | bytes 786448 | tf_op jit(solution)/shard_map/while/body/eval_jaxpr/reduce_scatter | solution.py:201
  411.9 28.6 %all-gather.17.cloned.1.call-done = bf16[1024,2,768]{2,0,1:T(8,128)(2,1)} async-done(((bf16[256,2,768]{2,0,1:T(8,128)(2,1)}), bf16[1024,2,768]{2,0,1:T(8,128)(2,1)}) %all-gather.17.cloned.1.call-update) | async-done | bytes 3145744 | tf_op jit(solution)/shard_map/while/body/eval_jaxpr/all_gather | solution.py:213
  440.5 11.1 convert_reduce_fusion.11
  457.7 37.7 %reduce-scatter.11.cloned.1.call-done = bf16[256,2,768]{2,0,1:T(8,128)(2,1)} async-done(((bf16[1024,2,768]{2,0,1:T(8,128)(2,1)}), bf16[256,2,768]{2,0,1:T(8,128)(2,1)}) %reduce-scatter.11.cloned.1.call-update) | async-done | bytes 786448 | tf_op jit(solution)/shard_map/while/body/eval_jaxpr/reduce_scatter | solution.py:222
  503.8 6.5 bitcast_convert_fusion.11
  510.4 21.5 %all-gather.19.cloned.1.call-done = bf16[1024,2,768]{2,0,1:T(8,128)(2,1)} async-done(((bf16[256,2,768]{2,0,1:T(8,128)(2,1)}), bf16[1024,2,768]{2,0,1:T(8,128)(2,1)}) %all-gather.19.cloned.1.call-update) | async-done | bytes 3145744 | tf_op jit(solution)/shard_map/while/body/eval_jaxpr/all_gather | solution.py:232
  535.8 6.4 fusion.278
  542.2 29.4 %fusion.282 = bf16[512,2,3,64]{0,3,2,1:T(8,128)(2,1)} fusion(f32[2,3,512,1024]{3,2,1,0:T(8,128)} %fusion.278, f32[2,3,512,1024]{3,2,1,0:T(8,128)} %copy-done.4, f32[2,3,512]{2,1,0:T(4,128)S(1)} %log_add_fusion.5, pred[2,512,1024]{2,1,0:T(8,128)(4,1)} %get-tuple-element.1089, bf16[1024,2,3,3,64]{0,4,3,2,1:T(8,128)(2,1)S(1)} %bitcast.312), kind=kOutput, calls=%fused_computation.130.clone.1 | convolution fusion | flops 437456896 | bytes 53641216 | tf_op jit(solution)/shard_map/while/body/eval_jaxpr/shqk,kshd->qshd/dot_general | solution.py:115
  571.6 24.2 %fusion.279 = f32[2,3,64,1024]{3,2,1,0:T(8,128)} fusion(f32[2,3,512,1024]{3,2,1,0:T(8,128)} %fusion.278, f32[2,3,512,1024]{3,2,1,0:T(8,128)} %copy-done.4, f32[2,3,512]{2,1,0:T(4,128)} %copy-done.38, pred[2,512,1024]{2,1,0:T(8,128)(4,1)} %get-tuple-element.1089, bf16[1024,2,3,3,64]{0,4,3,2,1:T(8,128)(2,1)} %bitcast.307), kind=kOutput, calls=%fused_computation.22.clone.1 | convolution fusion | flops 437260288 | bytes 54427648 | tf_op jit(solution)/shard_map/while/body/eval_jaxpr/shqk,qshd->kshd/dot_general | solution.py:119
  599.5 5.5 all-to-all-start.1
  605.1 7.8 fusion.280
  613.0 6.7 fusion.277
  624.2 26.9 %fusion.281 = bf16[512,2,3,64]{0,3,2,1:T(8,128)(2,1)} fusion(f32[2,3,512,1024]{3,2,1,0:T(8,128)} %fusion.280, f32[2,3,512,1024]{3,2,1,0:T(8,128)} %copy-done.3, f32[2,3,512]{2,1,0:T(4,128)S(1)} %copy-done.37, pred[2,512,1024]{2,1,0:T(8,128)(4,1)S(1)} %copy-done.10, bf16[1024,2,3,3,64]{0,4,3,2,1:T(8,128)(2,1)} %bitcast.309), kind=kOutput, calls=%fused_computation.131.clone.1 | convolution fusion | flops 437456896 | bytes 53641216 | tf_op jit(solution)/shard_map/while/body/eval_jaxpr/shqk,kshd->qshd/dot_general | solution.py:115
  651.1 24.7 %add_convert_fusion.16 = bf16[2,3,64,1024]{3,2,1,0:T(8,128)(2,1)} fusion(f32[2,3,64,1024]{3,2,1,0:T(8,128)} %fusion.279, f32[2,3,512,1024]{3,2,1,0:T(8,128)} %fusion.280, f32[2,3,512,1024]{3,2,1,0:T(8,128)} %copy-done.3, f32[2,3,512]{2,1,0:T(4,128)} %log_add_fusion.4, pred[2,512,1024]{2,1,0:T(8,128)(4,1)} %copy-done.9, ...), kind=kOutput, calls=%fused_computation.104.clone.1 | convolution fusion | flops 438046720 | bytes 55214080 | tf_op jit(solution)/shard_map/while/body/eval_jaxpr/shqk,qshd->kshd/dot_general | solution.py:119
  677.8 5.8 bitcast_convert_fusion.8
  683.6 6.7 bitcast_convert_fusion.9
  701.4 6.4 all-to-all-start
  719.8 37.5 %all-to-all-done = bf16[8,96,1344]{2,1,0:T(8,128)(2,1)} async-done(((bf16[8,96,1344]{2,1,0:T(8,128)(2,1)}), bf16[8,96,1344]{2,1,0:T(8,128)(2,1)}, u32[]{:S(2)}, u32[]{:S(2)}) %all-to-all-start) | async-done | bytes 2064416 | tf_op jit(solution)/shard_map/while/body/eval_jaxpr/all_to_all | solution.py:24
  767.6 38.2 %all_gather.97 = bf16[768,3,192]{2,1,0:T(4,128)(2,1)S(1)} all-gather(bf16[96,3,192]{2,1,0:T(4,128)(2,1)} %get-tuple-element.1198), channel_id=1, replica_groups=mesh['dp'=8,'tensor'=4] {'dp'}, dimensions={0}, use_global_device_ids=true | all-gather | bytes 995328 | tf_op jit(solution)/shard_map/while/body/eval_jaxpr/all_gather | solution.py:141
  808.2 33.2 %all_gather.98 = bf16[192,768]{0,1:T(8,128)(2,1)} all-gather(bf16[192,96]{0,1:T(8,128)(2,1)} %get-tuple-element.1202), channel_id=1, replica_groups=mesh['dp'=8,'tensor'=4] {'dp'}, dimensions={1}, use_global_device_ids=true | all-gather | bytes 331776 | tf_op jit(solution)/shard_map/while/body/eval_jaxpr/all_gather | solution.py:145
  855.0 7.1 fusion.264
  862.1 5.3 fusion.266
  867.4 5.3 fusion.265
  878.8 33.5 %reduce-scatter.7.cloned.1.call-done = bf16[256,2,768]{2,0,1:T(8,128)(2,1)} async-done(((bf16[1024,2,768]{2,0,1:T(8,128)(2,1)}), bf16[256,2,768]{2,0,1:T(8,128)(2,1)}) %reduce-scatter.7.cloned.1.call-update) | async-done | bytes 786448 | tf_op jit(solution)/shard_map/while/body/eval_jaxpr/reduce_scatter | solution.py:183
  918.6 37.1 %all-gather.13.cloned.1.call-done = bf16[768,768]{1,0:T(8,128)(2,1)} async-done(((bf16[96,768]{1,0:T(8,128)(2,1)}), bf16[768,768]{1,0:T(8,128)(2,1)}) %all-gather.13.cloned.1.call-update) | async-done | bytes 1179664 | tf_op jit(solution)/shard_map/while/body/eval_jaxpr/all_gather | solution.py:142
  955.7 28.7 %all-gather.11.cloned.1.call-done = bf16[1024,2,768]{2,0,1:T(8,128)(2,1)} async-done(((bf16[256,2,768]{2,0,1:T(8,128)(2,1)}), bf16[1024,2,768]{2,0,1:T(8,128)(2,1)}) %all-gather.11.cloned.1.call-update) | async-done | bytes 3145744 | tf_op jit(solution)/shard_map/while/body/eval_jaxpr/all_gather | solution.py:193
  984.3 6.7 fusion.270
  993.7 15.7 %multiply_convert_fusion.4 = (bf16[1024,2,768]{2,0,1:T(8,128)(2,1)}, f32[1024,2,768]{2,0,1:T(8,128)}) fusion(f32[1024,2,768]{2,0,1:T(8,128)S(1)} %get-tuple-element.1095, f32[768]{0:T(1024)S(1)} %get-tuple-element.1207, u8[1024,768]{1,0:T(8,128)(4,1)S(1)} %get-tuple-element.1096, u8[1024,768]{1,0:T(8,128)(4,1)S(1)} %get-tuple-element.1097), kind=kLoop, calls=%fused_computation.40.clone.1 | loop fusion | flops 111673344 | bytes 17304576 | tf_op jit(solution)/shard_map/while/body/eval_jaxpr/convert_element_type | solution.py:199
  1009.5 18.0 %all-gather.15.cloned.1.call-done = bf16[768,768]{0,1:T(8,128)(2,1)} async-done(((bf16[768,96]{0,1:T(8,128)(2,1)}), bf16[768,768]{0,1:T(8,128)(2,1)}) %all-gather.15.cloned.1.call-update) | async-done | bytes 1179664 | tf_op jit(solution)/shard_map/while/body/eval_jaxpr/all_gather | solution.py:146
  1027.5 6.6 convolution_convert_fusion.9
  1037.4 33.4 %reduce-scatter.9.cloned.1.call-done = bf16[256,2,768]{2,0,1:T(8,128)(2,1)} async-done(((bf16[1024,2,768]{2,0,1:T(8,128)(2,1)}), bf16[256,2,768]{2,0,1:T(8,128)(2,1)}) %reduce-scatter.9.cloned.1.call-update) | async-done | bytes 786448 | tf_op jit(solution)/shard_map/while/body/eval_jaxpr/reduce_scatter | solution.py:201
  1077.6 28.6 %all-gather.17.cloned.1.call-done = bf16[1024,2,768]{2,0,1:T(8,128)(2,1)} async-done(((bf16[256,2,768]{2,0,1:T(8,128)(2,1)}), bf16[1024,2,768]{2,0,1:T(8,128)(2,1)}) %all-gather.17.cloned.1.call-update) | async-done | bytes 3145744 | tf_op jit(solution)/shard_map/while/body/eval_jaxpr/all_gather | solution.py:213
  1106.2 11.1 convert_reduce_fusion.11
  1123.7 37.5 %reduce-scatter.11.cloned.1.call-done = bf16[256,2,768]{2,0,1:T(8,128)(2,1)} async-done(((bf16[1024,2,768]{2,0,1:T(8,128)(2,1)}), bf16[256,2,768]{2,0,1:T(8,128)(2,1)}) %reduce-scatter.11.cloned.1.call-update) | async-done | bytes 786448 | tf_op jit(solution)/shard_map/while/body/eval_jaxpr/reduce_scatter | solution.py:222
  1169.6 6.5 bitcast_convert_fusion.11
  1176.1 21.5 %all-gather.19.cloned.1.call-done = bf16[1024,2,768]{2,0,1:T(8,128)(2,1)} async-done(((bf16[256,2,768]{2,0,1:T(8,128)(2,1)}), bf16[1024,2,768]{2,0,1:T(8,128)(2,1)}) %all-gather.19.cloned.1.call-update) | async-done | bytes 3145744 | tf_op jit(solution)/shard_map/while/body/eval_jaxpr/all_gather | solution.py:232
  1201.5 6.4 fusion.278
  1207.9 29.1 %fusion.282 = bf16[512,2,3,64]{0,3,2,1:T(8,128)(2,1)} fusion(f32[2,3,512,1024]{3,2,1,0:T(8,128)} %fusion.278, f32[2,3,512,1024]{3,2,1,0:T(8,128)} %copy-done.4, f32[2,3,512]{2,1,0:T(4,128)S(1)} %log_add_fusion.5, pred[2,512,1024]{2,1,0:T(8,128)(4,1)} %get-tuple-element.1089, bf16[1024,2,3,3,64]{0,4,3,2,1:T(8,128)(2,1)S(1)} %bitcast.312), kind=kOutput, calls=%fused_computation.130.clone.1 | convolution fusion | flops 437456896 | bytes 53641216 | tf_op jit(solution)/shard_map/while/body/eval_jaxpr/shqk,kshd->qshd/dot_general | solution.py:115
  1237.0 24.2 %fusion.279 = f32[2,3,64,1024]{3,2,1,0:T(8,128)} fusion(f32[2,3,512,1024]{3,2,1,0:T(8,128)} %fusion.278, f32[2,3,512,1024]{3,2,1,0:T(8,128)} %copy-done.4, f32[2,3,512]{2,1,0:T(4,128)} %copy-done.38, pred[2,512,1024]{2,1,0:T(8,128)(4,1)} %get-tuple-element.1089, bf16[1024,2,3,3,64]{0,4,3,2,1:T(8,128)(2,1)} %bitcast.307), kind=kOutput, calls=%fused_computation.22.clone.1 | convolution fusion | flops 437260288 | bytes 54427648 | tf_op jit(solution)/shard_map/while/body/eval_jaxpr/shqk,qshd->kshd/dot_general | solution.py:119
  1265.0 5.5 all-to-all-start.1
  1270.6 7.8 fusion.280
  1278.4 6.8 fusion.277
  1289.7 26.9 %fusion.281 = bf16[512,2,3,64]{0,3,2,1:T(8,128)(2,1)} fusion(f32[2,3,512,1024]{3,2,1,0:T(8,128)} %fusion.280, f32[2,3,512,1024]{3,2,1,0:T(8,128)} %copy-done.3, f32[2,3,512]{2,1,0:T(4,128)S(1)} %copy-done.37, pred[2,512,1024]{2,1,0:T(8,128)(4,1)S(1)} %copy-done.10, bf16[1024,2,3,3,64]{0,4,3,2,1:T(8,128)(2,1)} %bitcast.309), kind=kOutput, calls=%fused_computation.131.clone.1 | convolution fusion | flops 437456896 | bytes 53641216 | tf_op jit(solution)/shard_map/while/body/eval_jaxpr/shqk,kshd->qshd/dot_general | solution.py:115
  1316.6 24.8 %add_convert_fusion.16 = bf16[2,3,64,1024]{3,2,1,0:T(8,128)(2,1)} fusion(f32[2,3,64,1024]{3,2,1,0:T(8,128)} %fusion.279, f32[2,3,512,1024]{3,2,1,0:T(8,128)} %fusion.280, f32[2,3,512,1024]{3,2,1,0:T(8,128)} %copy-done.3, f32[2,3,512]{2,1,0:T(4,128)} %log_add_fusion.4, pred[2,512,1024]{2,1,0:T(8,128)(4,1)} %copy-done.9, ...), kind=kOutput, calls=%fused_computation.104.clone.1 | convolution fusion | flops 438046720 | bytes 55214080 | tf_op jit(solution)/shard_map/while/body/eval_jaxpr/shqk,qshd->kshd/dot_general | solution.py:119
  1343.3 5.8 bitcast_convert_fusion.8
  1349.2 6.7 bitcast_convert_fusion.9
  1366.9 6.6 all-to-all-start
  1387.4 35.6 %all-to-all-done = bf16[8,96,1344]{2,1,0:T(8,128)(2,1)} async-done(((bf16[8,96,1344]{2,1,0:T(8,128)(2,1)}), bf16[8,96,1344]{2,1,0:T(8,128)(2,1)}, u32[]{:S(2)}, u32[]{:S(2)}) %all-to-all-start) | async-done | bytes 2064416 | tf_op jit(solution)/shard_map/while/body/eval_jaxpr/all_to_all | solution.py:24
  1430.5 38.2 %all-reduce.2 = (f32[10,768]{1,0:T(8,128)S(1)}, f32[2,768]{1,0:T(2,128)S(1)}) all-reduce(f32[10,768]{1,0:T(8,128)} %get-tuple-element.601, f32[2,768]{1,0:T(2,128)} %get-tuple-element.602), channel_id=6, replica_groups=mesh['dp'=8,'tensor'=4] {'dp','tensor'}, use_global_device_ids=true, to_apply=%region_31.0.clone | all-reduce | flops 9216 | bytes 73728
  (478 shorter events, 219.2 us)
Async XLA Ops:
  96.3 113.9 %copy-start.47 = (f32[1,768]{1,0:T(1,128)}, f32[1,768]{1,0:T(1,128)S(1)}, u32[]{:S(2)}) copy-start(f32[1,768]{1,0:T(1,128)S(1)} %get-tuple-element.1204) | copy-start | bytes 9220 | tf_op jit(solution)/shard_map/while
  96.3 272.3 %copy-start.45 = (f32[1,768]{1,0:T(1,128)}, f32[1,768]{1,0:T(1,128)S(1)}, u32[]{:S(2)}) copy-start(f32[1,768]{1,0:T(1,128)S(1)} %get-tuple-element.1210) | copy-start | bytes 9220 | tf_op jit(solution)/shard_map/while
  96.4 272.3 %copy-start.49 = (f32[1,768]{1,0:T(1,128)}, f32[1,768]{1,0:T(1,128)S(1)}, u32[]{:S(2)}) copy-start(f32[1,768]{1,0:T(1,128)S(1)} %get-tuple-element.1211) | copy-start | bytes 9220 | tf_op jit(solution)/shard_map/while
  96.4 344.1 %copy-start.43 = (f32[768]{0:T(1024)}, f32[768]{0:T(1024)S(1)}, u32[]{:S(2)}) copy-start(f32[768]{0:T(1024)S(1)} %get-tuple-element.1207) | copy-start | bytes 9220 | tf_op jit(solution)/shard_map/while
  96.4 79.9 %all-gather.9.cloned.1.call-start = ((), (), s32[]{:S(2)}) async-start(), calls=%async_computation.6 | async-start | bytes 3932160 | tf_op jit(solution)/shard_map/while/body/eval_jaxpr/all_gather | solution.py:170
  99.6 146.9 %reduce-scatter.7.cloned.1.call-start = ((), (), s32[]{:S(2)}) async-start(), calls=%async_computation.7 | async-start | bytes 3932160 | tf_op jit(solution)/shard_map/while/body/eval_jaxpr/reduce_scatter | solution.py:183
  137.4 43.4 %copy-start.7 = (bf16[768,3,192]{2,1,0:T(4,128)(2,1)}, bf16[768,3,192]{2,1,0:T(4,128)(2,1)S(1)}, u32[]{:S(2)}) copy-start(bf16[768,3,192]{2,1,0:T(4,128)(2,1)S(1)} %all_gather.97) | copy-start | bytes 2654212 | tf_op jit(solution)/shard_map/while
  208.8 81.1 %all-gather.13.cloned.1.call-start = ((), (), s32[]{:S(2)}) async-start(), calls=%async_computation.9 | async-start | bytes 1327104 | tf_op jit(solution)/shard_map/while/body/eval_jaxpr/all_gather | solution.py:142
  209.5 109.1 %all-gather.11.cloned.1.call-start = ((), (), s32[]{:S(2)}) async-start(), calls=%async_computation.8 | async-start | bytes 3932160 | tf_op jit(solution)/shard_map/while/body/eval_jaxpr/all_gather | solution.py:193
  252.0 109.8 %all-gather.15.cloned.1.call-start = ((), (), s32[]{:S(2)}) async-start(), calls=%async_computation.10 | async-start | bytes 1327104 | tf_op jit(solution)/shard_map/while/body/eval_jaxpr/all_gather | solution.py:146
  252.6 152.5 %reduce-scatter.9.cloned.1.call-start = ((), (), s32[]{:S(2)}) async-start(), calls=%async_computation.11 | async-start | bytes 3932160 | tf_op jit(solution)/shard_map/while/body/eval_jaxpr/reduce_scatter | solution.py:201
  368.4 36.8 %copy-start = (bf16[256,2,768]{2,0,1:T(8,128)(2,1)S(1)}, bf16[256,2,768]{2,0,1:T(8,128)(2,1)}, u32[]{:S(2)}) copy-start(bf16[256,2,768]{2,0,1:T(8,128)(2,1)} %reduce-scatter.7.cloned.1.call-done) | copy-start | bytes 2359300 | tf_op jit(solution)/shard_map/while
  368.4 72.1 %all-gather.17.cloned.1.call-start = ((), (), s32[]{:S(2)}) async-start(), calls=%async_computation.12 | async-start | bytes 3932160 | tf_op jit(solution)/shard_map/while/body/eval_jaxpr/all_gather | solution.py:213
  371.6 36.3 %copy-start.5 = (bf16[256,2,768]{2,1,0:T(2,128)(2,1)}, bf16[256,2,768]{2,1,0:T(2,128)(2,1)S(1)}, u32[]{:S(2)}) copy-start(bf16[256,2,768]{2,1,0:T(2,128)(2,1)S(1)} %constant_dynamic-slice_fusion.9) | copy-start | bytes 2359300 | tf_op jit(solution)/shard_map/while
  411.8 83.6 %reduce-scatter.11.cloned.1.call-start = ((), (), s32[]{:S(2)}) async-start(), calls=%async_computation.13 | async-start | bytes 3932160 | tf_op jit(solution)/shard_map/while/body/eval_jaxpr/reduce_scatter | solution.py:222
  457.4 74.5 %all-gather.19.cloned.1.call-start = ((), (), s32[]{:S(2)}) async-start(), calls=%async_computation.14 | async-start | bytes 3932160 | tf_op jit(solution)/shard_map/while/body/eval_jaxpr/all_gather | solution.py:232
  503.2 28.7 %copy-start.14 = (bf16[192,768]{0,1:T(8,128)(2,1)S(1)}, bf16[192,768]{0,1:T(8,128)(2,1)}, u32[]{:S(2)}) copy-start(bf16[192,768]{0,1:T(8,128)(2,1)} %all_gather.98) | copy-start | bytes 884740 | tf_op jit(solution)/shard_map/while
  503.8 38.3 %copy-start.38 = (f32[2,3,512]{2,1,0:T(4,128)}, f32[2,3,512]{2,1,0:T(4,128)S(1)}, u32[]{:S(2)}) copy-start(f32[2,3,512]{2,1,0:T(4,128)S(1)} %log_add_fusion.5) | copy-start | bytes 36868 | tf_op jit(solution)/shard_map/while
  510.4 25.4 %copy-start.23 = (bf16[1024,2,3,192]{0,3,2,1:T(8,128)(2,1)S(1)}, bf16[1024,2,3,192]{0,3,2,1:T(8,128)(2,1)}, u32[]{:S(2)}) copy-start(bf16[1024,2,3,192]{0,3,2,1:T(8,128)(2,1)} %copy-done.22) | copy-start | bytes 7077892 | tf_op jit(solution)/shard_map/while
  599.5 101.9 %all-to-all-start.1 = ((bf16[8,960,96]{1,2,0:T(8,128)(2,1)}), bf16[8,960,96]{1,2,0:T(8,128)(2,1)S(1)}, u32[]{:S(2)}, u32[]{:S(2)}) async-start(bf16[8,960,96]{1,2,0:T(8,128)(2,1)} %bitcast.285), calls=%async_computation.5 | async-start | bytes 3145728 | tf_op jit(solution)/shard_map/while/body/eval_jaxpr/all_to_all | solution.py:24
  605.0 154.7 %reduce-scatter.13.cloned.1.call-start = ((), (), s32[]{:S(2)}) async-start(), calls=%async_computation.15 | async-start | bytes 3932160 | tf_op jit(solution)/shard_map/while/body/eval_jaxpr/reduce_scatter | solution.py:252
  651.1 24.8 %copy-start.28 = (bf16[512,2,3,64]{0,3,2,1:T(8,128)(2,1)S(1)}, bf16[512,2,3,64]{0,3,2,1:T(8,128)(2,1)}, u32[]{:S(2)}) copy-start(bf16[512,2,3,64]{0,3,2,1:T(8,128)(2,1)} %fusion.282) | copy-start | bytes 1179652 | tf_op jit(solution)/shard_map/while
  651.1 26.7 %copy-start.8 = (bf16[768,3,192]{2,1,0:T(4,128)(2,1)S(1)}, bf16[768,3,192]{2,1,0:T(4,128)(2,1)}, u32[]{:S(2)}) copy-start(bf16[768,3,192]{2,1,0:T(4,128)(2,1)} %copy-done.7) | copy-start | bytes 2654212 | tf_op jit(solution)/shard_map/while
  701.4 55.9 %all-to-all-start = ((bf16[8,96,1344]{2,1,0:T(8,128)(2,1)}), bf16[8,96,1344]{2,1,0:T(8,128)(2,1)}, u32[]{:S(2)}, u32[]{:S(2)}) async-start(bf16[8,96,1344]{2,1,0:T(8,128)(2,1)} %pad_maximum_fusion.20), calls=%async_computation.4 | async-start | bytes 4325376 | tf_op jit(solution)/shard_map/while/body/eval_jaxpr/all_to_all | solution.py:24
  712.7 46.9 %copy-start.26 = (f32[96,3,192]{0,2,1:T(8,128)S(1)}, f32[96,3,192]{0,2,1:T(8,128)}, u32[]{:S(2)}) copy-start(f32[96,3,192]{0,2,1:T(8,128)} %get-tuple-element.1157) | copy-start | bytes 663556 | tf_op jit(solution)/shard_map/while
  713.1 46.7 %copy-start.2 = (f32[256,2,768]{2,0,1:T(8,128)S(1)}, f32[256,2,768]{2,0,1:T(8,128)}, u32[]{:S(2)}) copy-start(f32[256,2,768]{2,0,1:T(8,128)} %copy-done.1) | copy-start | bytes 4718596 | tf_op jit(solution)/shard_map/while
  717.9 43.3 %copy-start.32 = (f32[10,768]{1,0:T(8,128)}, f32[10,768]{1,0:T(8,128)S(1)}, u32[]{:S(2)}) copy-start(f32[10,768]{1,0:T(8,128)S(1)} %select_add_fusion.5) | copy-start | bytes 92164 | tf_op jit(solution)/shard_map/while
  718.2 41.2 %copy-start.29 = (f32[96,768]{1,0:T(8,128)S(1)}, f32[96,768]{1,0:T(8,128)}, u32[]{:S(2)}) copy-start(f32[96,768]{1,0:T(8,128)} %get-tuple-element.1158) | copy-start | bytes 884740 | tf_op jit(solution)/shard_map/while
  719.8 43.2 %copy-start.44 = (f32[768]{0:T(1024)S(1)}, f32[768]{0:T(1024)}, u32[]{:S(2)}) copy-start(f32[768]{0:T(1024)} %copy-done.43) | copy-start | bytes 9220 | tf_op jit(solution)/shard_map/while
  719.8 43.2 %copy-start.46 = (f32[1,768]{1,0:T(1,128)S(1)}, f32[1,768]{1,0:T(1,128)}, u32[]{:S(2)}) copy-start(f32[1,768]{1,0:T(1,128)} %copy-done.45) | copy-start | bytes 9220 | tf_op jit(solution)/shard_map/while
  719.8 43.2 %copy-start.48 = (f32[1,768]{1,0:T(1,128)S(1)}, f32[1,768]{1,0:T(1,128)}, u32[]{:S(2)}) copy-start(f32[1,768]{1,0:T(1,128)} %copy-done.47) | copy-start | bytes 9220 | tf_op jit(solution)/shard_map/while
  719.8 43.2 %copy-start.50 = (f32[1,768]{1,0:T(1,128)S(1)}, f32[1,768]{1,0:T(1,128)}, u32[]{:S(2)}) copy-start(f32[1,768]{1,0:T(1,128)} %copy-done.49) | copy-start | bytes 9220 | tf_op jit(solution)/shard_map/while
  763.5 114.6 %copy-start.47 = (f32[1,768]{1,0:T(1,128)}, f32[1,768]{1,0:T(1,128)S(1)}, u32[]{:S(2)}) copy-start(f32[1,768]{1,0:T(1,128)S(1)} %get-tuple-element.1204) | copy-start | bytes 9220 | tf_op jit(solution)/shard_map/while
  763.5 270.9 %copy-start.45 = (f32[1,768]{1,0:T(1,128)}, f32[1,768]{1,0:T(1,128)S(1)}, u32[]{:S(2)}) copy-start(f32[1,768]{1,0:T(1,128)S(1)} %get-tuple-element.1210) | copy-start | bytes 9220 | tf_op jit(solution)/shard_map/while
  763.5 271.0 %copy-start.49 = (f32[1,768]{1,0:T(1,128)}, f32[1,768]{1,0:T(1,128)S(1)}, u32[]{:S(2)}) copy-start(f32[1,768]{1,0:T(1,128)S(1)} %get-tuple-element.1211) | copy-start | bytes 9220 | tf_op jit(solution)/shard_map/while
  763.5 342.7 %copy-start.43 = (f32[768]{0:T(1024)}, f32[768]{0:T(1024)S(1)}, u32[]{:S(2)}) copy-start(f32[768]{0:T(1024)S(1)} %get-tuple-element.1207) | copy-start | bytes 9220 | tf_op jit(solution)/shard_map/while
  763.5 81.1 %all-gather.9.cloned.1.call-start = ((), (), s32[]{:S(2)}) async-start(), calls=%async_computation.6 | async-start | bytes 3932160 | tf_op jit(solution)/shard_map/while/body/eval_jaxpr/all_gather | solution.py:170
  766.8 145.5 %reduce-scatter.7.cloned.1.call-start = ((), (), s32[]{:S(2)}) async-start(), calls=%async_computation.7 | async-start | bytes 3932160 | tf_op jit(solution)/shard_map/while/body/eval_jaxpr/reduce_scatter | solution.py:183
  805.7 43.4 %copy-start.7 = (bf16[768,3,192]{2,1,0:T(4,128)(2,1)}, bf16[768,3,192]{2,1,0:T(4,128)(2,1)S(1)}, u32[]{:S(2)}) copy-start(bf16[768,3,192]{2,1,0:T(4,128)(2,1)S(1)} %all_gather.97) | copy-start | bytes 2654212 | tf_op jit(solution)/shard_map/while
  876.6 79.0 %all-gather.13.cloned.1.call-start = ((), (), s32[]{:S(2)}) async-start(), calls=%async_computation.9 | async-start | bytes 1327104 | tf_op jit(solution)/shard_map/while/body/eval_jaxpr/all_gather | solution.py:142
  877.4 106.9 %all-gather.11.cloned.1.call-start = ((), (), s32[]{:S(2)}) async-start(), calls=%async_computation.8 | async-start | bytes 3932160 | tf_op jit(solution)/shard_map/while/body/eval_jaxpr/all_gather | solution.py:193
  917.7 109.8 %all-gather.15.cloned.1.call-start = ((), (), s32[]{:S(2)}) async-start(), calls=%async_computation.10 | async-start | bytes 1327104 | tf_op jit(solution)/shard_map/while/body/eval_jaxpr/all_gather | solution.py:146
  918.3 152.5 %reduce-scatter.9.cloned.1.call-start = ((), (), s32[]{:S(2)}) async-start(), calls=%async_computation.11 | async-start | bytes 3932160 | tf_op jit(solution)/shard_map/while/body/eval_jaxpr/reduce_scatter | solution.py:201
  1034.1 36.8 %copy-start = (bf16[256,2,768]{2,0,1:T(8,128)(2,1)S(1)}, bf16[256,2,768]{2,0,1:T(8,128)(2,1)}, u32[]{:S(2)}) copy-start(bf16[256,2,768]{2,0,1:T(8,128)(2,1)} %reduce-scatter.7.cloned.1.call-done) | copy-start | bytes 2359300 | tf_op jit(solution)/shard_map/while
  1034.1 72.1 %all-gather.17.cloned.1.call-start = ((), (), s32[]{:S(2)}) async-start(), calls=%async_computation.12 | async-start | bytes 3932160 | tf_op jit(solution)/shard_map/while/body/eval_jaxpr/all_gather | solution.py:213
  1037.4 36.3 %copy-start.5 = (bf16[256,2,768]{2,1,0:T(2,128)(2,1)}, bf16[256,2,768]{2,1,0:T(2,128)(2,1)S(1)}, u32[]{:S(2)}) copy-start(bf16[256,2,768]{2,1,0:T(2,128)(2,1)S(1)} %constant_dynamic-slice_fusion.9) | copy-start | bytes 2359300 | tf_op jit(solution)/shard_map/while
  1077.5 83.6 %reduce-scatter.11.cloned.1.call-start = ((), (), s32[]{:S(2)}) async-start(), calls=%async_computation.13 | async-start | bytes 3932160 | tf_op jit(solution)/shard_map/while/body/eval_jaxpr/reduce_scatter | solution.py:222
  1123.1 74.5 %all-gather.19.cloned.1.call-start = ((), (), s32[]{:S(2)}) async-start(), calls=%async_computation.14 | async-start | bytes 3932160 | tf_op jit(solution)/shard_map/while/body/eval_jaxpr/all_gather | solution.py:232
  1168.9 28.7 %copy-start.14 = (bf16[192,768]{0,1:T(8,128)(2,1)S(1)}, bf16[192,768]{0,1:T(8,128)(2,1)}, u32[]{:S(2)}) copy-start(bf16[192,768]{0,1:T(8,128)(2,1)} %all_gather.98) | copy-start | bytes 884740 | tf_op jit(solution)/shard_map/while
  1169.6 38.3 %copy-start.38 = (f32[2,3,512]{2,1,0:T(4,128)}, f32[2,3,512]{2,1,0:T(4,128)S(1)}, u32[]{:S(2)}) copy-start(f32[2,3,512]{2,1,0:T(4,128)S(1)} %log_add_fusion.5) | copy-start | bytes 36868 | tf_op jit(solution)/shard_map/while
  1176.1 25.4 %copy-start.23 = (bf16[1024,2,3,192]{0,3,2,1:T(8,128)(2,1)S(1)}, bf16[1024,2,3,192]{0,3,2,1:T(8,128)(2,1)}, u32[]{:S(2)}) copy-start(bf16[1024,2,3,192]{0,3,2,1:T(8,128)(2,1)} %copy-done.22) | copy-start | bytes 7077892 | tf_op jit(solution)/shard_map/while
  1265.0 102.0 %all-to-all-start.1 = ((bf16[8,960,96]{1,2,0:T(8,128)(2,1)}), bf16[8,960,96]{1,2,0:T(8,128)(2,1)S(1)}, u32[]{:S(2)}, u32[]{:S(2)}) async-start(bf16[8,960,96]{1,2,0:T(8,128)(2,1)} %bitcast.285), calls=%async_computation.5 | async-start | bytes 3145728 | tf_op jit(solution)/shard_map/while/body/eval_jaxpr/all_to_all | solution.py:24
  1270.5 155.0 %reduce-scatter.13.cloned.1.call-start = ((), (), s32[]{:S(2)}) async-start(), calls=%async_computation.15 | async-start | bytes 3932160 | tf_op jit(solution)/shard_map/while/body/eval_jaxpr/reduce_scatter | solution.py:252
  1316.6 24.8 %copy-start.28 = (bf16[512,2,3,64]{0,3,2,1:T(8,128)(2,1)S(1)}, bf16[512,2,3,64]{0,3,2,1:T(8,128)(2,1)}, u32[]{:S(2)}) copy-start(bf16[512,2,3,64]{0,3,2,1:T(8,128)(2,1)} %fusion.282) | copy-start | bytes 1179652 | tf_op jit(solution)/shard_map/while
  1316.6 26.8 %copy-start.8 = (bf16[768,3,192]{2,1,0:T(4,128)(2,1)S(1)}, bf16[768,3,192]{2,1,0:T(4,128)(2,1)}, u32[]{:S(2)}) copy-start(bf16[768,3,192]{2,1,0:T(4,128)(2,1)} %copy-done.7) | copy-start | bytes 2654212 | tf_op jit(solution)/shard_map/while
  1366.9 56.1 %all-to-all-start = ((bf16[8,96,1344]{2,1,0:T(8,128)(2,1)}), bf16[8,96,1344]{2,1,0:T(8,128)(2,1)}, u32[]{:S(2)}, u32[]{:S(2)}) async-start(bf16[8,96,1344]{2,1,0:T(8,128)(2,1)} %pad_maximum_fusion.20), calls=%async_computation.4 | async-start | bytes 4325376 | tf_op jit(solution)/shard_map/while/body/eval_jaxpr/all_to_all | solution.py:24
  1378.4 46.9 %copy-start.26 = (f32[96,3,192]{0,2,1:T(8,128)S(1)}, f32[96,3,192]{0,2,1:T(8,128)}, u32[]{:S(2)}) copy-start(f32[96,3,192]{0,2,1:T(8,128)} %get-tuple-element.1157) | copy-start | bytes 663556 | tf_op jit(solution)/shard_map/while
  1378.8 46.7 %copy-start.2 = (f32[256,2,768]{2,0,1:T(8,128)S(1)}, f32[256,2,768]{2,0,1:T(8,128)}, u32[]{:S(2)}) copy-start(f32[256,2,768]{2,0,1:T(8,128)} %copy-done.1) | copy-start | bytes 4718596 | tf_op jit(solution)/shard_map/while
  1383.7 43.3 %copy-start.32 = (f32[10,768]{1,0:T(8,128)}, f32[10,768]{1,0:T(8,128)S(1)}, u32[]{:S(2)}) copy-start(f32[10,768]{1,0:T(8,128)S(1)} %select_add_fusion.5) | copy-start | bytes 92164 | tf_op jit(solution)/shard_map/while
  1384.0 41.2 %copy-start.29 = (f32[96,768]{1,0:T(8,128)S(1)}, f32[96,768]{1,0:T(8,128)}, u32[]{:S(2)}) copy-start(f32[96,768]{1,0:T(8,128)} %get-tuple-element.1158) | copy-start | bytes 884740 | tf_op jit(solution)/shard_map/while
  1387.4 41.3 %copy-start.44 = (f32[768]{0:T(1024)S(1)}, f32[768]{0:T(1024)}, u32[]{:S(2)}) copy-start(f32[768]{0:T(1024)} %copy-done.43) | copy-start | bytes 9220 | tf_op jit(solution)/shard_map/while
  1387.4 41.3 %copy-start.46 = (f32[1,768]{1,0:T(1,128)S(1)}, f32[1,768]{1,0:T(1,128)}, u32[]{:S(2)}) copy-start(f32[1,768]{1,0:T(1,128)} %copy-done.45) | copy-start | bytes 9220 | tf_op jit(solution)/shard_map/while
  1387.4 41.3 %copy-start.48 = (f32[1,768]{1,0:T(1,128)S(1)}, f32[1,768]{1,0:T(1,128)}, u32[]{:S(2)}) copy-start(f32[1,768]{1,0:T(1,128)} %copy-done.47) | copy-start | bytes 9220 | tf_op jit(solution)/shard_map/while
  1387.4 41.3 %copy-start.50 = (f32[1,768]{1,0:T(1,128)S(1)}, f32[1,768]{1,0:T(1,128)}, u32[]{:S(2)}) copy-start(f32[1,768]{1,0:T(1,128)} %copy-done.49) | copy-start | bytes 9220 | tf_op jit(solution)/shard_map/while
  (78 other events, 678.2 us)
Sparse Core Ops, SparseCore 0:
  99.8 25.9 all-gather.8
  208.9 37.6 reduce-scatter.6
  248.8 41.1 all-gather.12
  291.3 27.1 all-gather.10
  320.6 41.1 all-gather.14
  368.5 36.5 reduce-scatter.8
  411.9 28.5 all-gather.16
  457.5 37.8 reduce-scatter.10
  503.3 28.4 all-gather.18
  683.7 38.2 reduce-scatter.12
  766.9 26.6 all-gather.8
  876.7 35.5 reduce-scatter.6
  914.5 41.1 all-gather.12
  957.1 27.1 all-gather.10
  986.3 41.1 all-gather.14
  1034.2 36.5 reduce-scatter.8
  1077.7 28.5 all-gather.16
  1123.3 37.8 reduce-scatter.10
  1169.1 28.4 all-gather.18
  1349.2 38.2 reduce-scatter.12
where the time goes:
time: 1480 us
  waiting for transfers between devices  555 us (38%)
  matrix products  420 us (28%)
  blocking collectives  261 us (18%)
  other arithmetic  121 us (8%)
  local copies, waits for them, and re-layouts  78.7 us (5%)
  starting transfers between devices  26.4 us (2%)
    dot_general x4, matrix products, attend_back(): jnp.einsum('shqk,kshd->qshd', scores_low, keys_all, preferred_element_typ...  112 us
    dot_general x4, matrix products, attend_back(): jnp.einsum('shqk,qshd->kshd', scores_low, query_block, preferred_element_...  97.8 us
    reduce_scatter x2, waiting for transfers between devices, micro_step(): lax.psum_scatter(jnp.einsum('psf,df->psd', row_block, mat_in, preferred_e...  75.3 us
    all_gather x2, blocking collectives, fetch_weights(): lax.all_gather(w_qkv, 'dp', axis=0, tiled=True)  75.1 us
    all_gather x2, waiting for transfers between devices, fetch_weights(): lax.all_gather(w_in, 'dp', axis=0, tiled=True)  74.2 us
    all_to_all x4, waiting for transfers between devices, sent_and_summed(): lax.all_to_all(blocks, axis, split_axis=0, concat_axis=0, tiled=True)  73.2 us
    reduce_scatter x2, waiting for transfers between devices, micro_step(): lax.psum_scatter(jnp.einsum('psh,hd->psd', row_block, mat_out, preferred_...  69.1 us
    reduce_scatter x2, waiting for transfers between devices, micro_step(): lax.psum_scatter(jnp.einsum('psf,fd->psd', row_block, mat_down, preferred...  66.9 us
  transfers between devices with their start and end apart: 24, of which 18 were waited for; matrix products, arithmetic and copies ran while one was open for 21% of the time, Pallas kernels for 0%

commit v1 on v0

v1 whole, which is shorter than its diff:
```python
import functools
import math

import jax
import jax.numpy as jnp
from jax import lax
from jax.experimental import pallas as pl
from jax.experimental.pallas import tpu as pltpu
from jax.sharding import PartitionSpec as P

f32=jnp.float32; bf16=jnp.bfloat16
L=1024; QB=256; NK=(512,512,768,1024)
C2=0.125*math.log2(math.e)
NEG=-1e30
def dotf(a,b): return jnp.dot(a,b,preferred_element_type=f32)
def dot_nt(a,b): return lax.dot_general(a,b,(((1,),(1,)),((),())),preferred_element_type=f32)
def masks(mask_ref, prefix):
    k=lax.broadcasted_iota(jnp.int32,(256,256),0); q=lax.broadcasted_iota(jnp.int32,(256,256),1)
    diag=k<=q
    mask_ref[0]=jnp.where(diag|(k<prefix),0.0,NEG)
    mask_ref[1]=jnp.where(k+256<prefix,0.0,NEG)+jnp.zeros((256,256),f32)
    mask_ref[2]=jnp.where(diag|(k+256<prefix),0.0,NEG)
    mask_ref[3]=jnp.where(diag,0.0,NEG)
MASKMAP={0:{0:0,1:1},1:{1:2},2:{2:3},3:{3:3}}
def masked(st,qb,mask_ref):
    parts=[]
    for kb in range(NK[qb]//256):
        p=st[kb*256:(kb+1)*256]
        mi=MASKMAP[qb].get(kb)
        parts.append(p if mi is None else p+mask_ref[mi])
    return jnp.concatenate(parts,0)
def fwd_kernel(prefix_ref,x_ref,w_ref,b_ref,proj_ref,projT_ref,heads_ref,ot_ref,lse_ref,zq_ref,mask_ref):
    masks(mask_ref,prefix_ref[0])
    proj=(dotf(x_ref[...],w_ref[:,:640])+b_ref[...]).astype(bf16)
    proj_ref[...]=proj
    projT_ref[...]=proj.T
    zq_ref[...]=jnp.zeros_like(zq_ref)
    for h in range(3):
        zq_ref[h,64+64*h:128+64*h,:]=projT_ref[64*h:64*h+64,:]
    ot_ref[...]=jnp.zeros_like(ot_ref)
    for h in range(3):
        for qb in range(4):
            nk=NK[qb]; qs=slice(qb*QB,qb*QB+QB)
            st=dotf(proj_ref[:nk,128:384],zq_ref[h,:,qs])
            st=masked(st,qb,mask_ref)
            m=jnp.max(st,axis=0,keepdims=True)
            p=jnp.exp2((st-m)*C2)
            l=jnp.sum(p,axis=0,keepdims=True)
            ot=dotf(projT_ref[384+64*h:448+64*h,:nk],p.astype(bf16))
            ot_ref[64+64*h:128+64*h,qs]=(ot/l).astype(bf16)
            lse_ref[h:h+1,qs]=m*C2+jnp.log2(l)
    heads_ref[...]=ot_ref[...].T
def attn_fwd(prefix,x,w1,bqkv):
    sq=pl.squeezed
    return pl.pallas_call(fwd_kernel,grid_spec=pltpu.PrefetchScalarGridSpec(num_scalar_prefetch=1,grid=(4,),
      in_specs=[pl.BlockSpec((L,768),lambda t,p:(0,0)),pl.BlockSpec((sq,768,768),lambda t,p:(t,0,0)),pl.BlockSpec((sq,1,640),lambda t,p:(t,0,0))],
      out_specs=[pl.BlockSpec((sq,L,640),lambda t,p:(t,0,0)),pl.BlockSpec((sq,640,L),lambda t,p:(t,0,0)),pl.BlockSpec((sq,L,256),lambda t,p:(t,0,0)),pl.BlockSpec((sq,256,L),lambda t,p:(t,0,0)),pl.BlockSpec((sq,8,L),lambda t,p:(t,0,0))],
      scratch_shapes=[pltpu.VMEM((3,256,L),bf16),pltpu.VMEM((4,256,256),f32)]),
      out_shape=[jax.ShapeDtypeStruct((4,L,640),bf16),jax.ShapeDtypeStruct((4,640,L),bf16),jax.ShapeDtypeStruct((4,L,256),bf16),jax.ShapeDtypeStruct((4,256,L),bf16),jax.ShapeDtypeStruct((4,8,L),f32)],
      compiler_params=pltpu.CompilerParams(vmem_limit_bytes=62<<20))(prefix,x,w1,bqkv)
def bwd_kernel(prefix_ref,g_ref,w_ref,proj_ref,projT_ref,ot_ref,lse_ref,gproj_ref,
               zq_ref,zdo_ref,qm_ref,dom_ref,pt_ref,ds_ref,mask_ref,gt_ref,dqt_ref):
    masks(mask_ref,prefix_ref[0])
    gh=dotf(g_ref[...],w_ref[:,512:768]).astype(bf16)
    gt_ref[...]=gh.T
    zq_ref[...]=jnp.zeros_like(zq_ref); zdo_ref[...]=jnp.zeros_like(zdo_ref)
    lane=lax.broadcasted_iota(jnp.int32,(1,256),1)
    for h in range(3):
        zq_ref[h,64+64*h:128+64*h,:]=projT_ref[64*h:64*h+64,:]
        zdo_ref[h,64*h:64*h+64,:]=gt_ref[64+64*h:128+64*h,:]*0.125
        sel=(lane>=64*h)&(lane<64*h+64)
        qm_ref[h]=jnp.where(sel,proj_ref[:,0:256],0)
        sel2=(lane>=64*h+64)&(lane<64*h+128)
        dom_ref[h]=jnp.where(sel2,gh,0)
    for h in range(3):
        d=jnp.sum(gt_ref[64+64*h:128+64*h,:].astype(f32)*ot_ref[64+64*h:128+64*h,:].astype(f32),axis=0,keepdims=True)*0.125
        for qb in range(4):
            nk=NK[qb]; qs=slice(qb*QB,qb*QB+QB)
            st=dotf(proj_ref[:nk,128:384],zq_ref[h,:,qs])
            st=masked(st,qb,mask_ref)
            p=jnp.exp2(st*C2-lse_ref[h:h+1,qs])
            dp=dotf(proj_ref[:nk,384:640],zdo_ref[h,:,qs])
            ds=(p*(dp-d[:,qs])).astype(bf16)
            pt_ref[h,:nk,qs]=p.astype(bf16)
            ds_ref[h,:nk,qs]=ds
            dqt_ref[64*h:64*h+64,qs]=dotf(projT_ref[192+64*h:256+64*h,:nk],ds).astype(bf16)
    gproj_ref[:,0:192]=dqt_ref[...].T
    for (k0,k1,q0) in ((0,512,0),(512,768,512),(768,1024,768)):
        dk=jnp.zeros((k1-k0,256),f32); dv=jnp.zeros((k1-k0,256),f32)
        for h in range(3):
            dk=dk+dotf(ds_ref[h,k0:k1,q0:],qm_ref[h,q0:,:])
            dv=dv+dotf(pt_ref[h,k0:k1,q0:],dom_ref[h,q0:,:])
        gproj_ref[k0:k1,192:384]=dk[:,0:192].astype(bf16)
        gproj_ref[k0:k1,384:576]=dv[:,64:256].astype(bf16)
    gproj_ref[:,576:640]=jnp.zeros((L,64),bf16)
def attn_bwd(prefix,g,w1,proj,projT,ot,lse):
    sq=pl.squeezed
    sp=lambda *s: pl.BlockSpec((sq,)+s,lambda t,p:(t,0,0))
    return pl.pallas_call(functools.partial(bwd_kernel),grid_spec=pltpu.PrefetchScalarGridSpec(num_scalar_prefetch=1,grid=(4,),
      in_specs=[pl.BlockSpec((L,768),lambda t,p:(0,0)),sp(768,768),sp(L,640),sp(640,L),sp(256,L),sp(8,L)],
      out_specs=sp(L,640),
      scratch_shapes=[pltpu.VMEM((3,256,L),bf16),pltpu.VMEM((3,256,L),bf16),pltpu.VMEM((3,L,256),bf16),pltpu.VMEM((3,L,256),bf16),pltpu.VMEM((3,L,L),bf16),pltpu.VMEM((3,L,L),bf16),pltpu.VMEM((4,256,256),f32),pltpu.VMEM((256,L),bf16),pltpu.VMEM((192,L),bf16)]),
      out_shape=jax.ShapeDtypeStruct((4,L,640),bf16),
      compiler_params=pltpu.CompilerParams(vmem_limit_bytes=62<<20))(prefix,g,w1,proj,projT,ot,lse)
MESH=pl.DeviceIdType.MESH
class Place:
    def __init__(self):
        dp=lax.axis_index("dp"); t=lax.axis_index("tensor")
        self.dp,self.t=dp,t
        self.z,self.x,self.y,self.c=dp//2,dp%2,t//2,t%2
    def peer(self,dim,j=1):
        return {'x':lambda:(self.dp^1,self.t),'z':lambda:(self.dp^(2*j),self.t),'y':lambda:(self.dp,self.t^2),'c':lambda:(self.dp,self.t^1)}[dim]()
    def peers_all(self):
        return [self.peer('x'),self.peer('y'),self.peer('c'),self.peer('z',1),self.peer('z',2),self.peer('z',3),(self.dp,self.t^3)]
def barrier(peers):
    b=pltpu.get_barrier_semaphore()
    for p in peers: pl.semaphore_signal(b,inc=1,device_id=p,device_id_type=MESH)
    pl.semaphore_wait(b,len(peers))
class Sems:
    def __init__(self,send,recv): self.s,self.r,self.n=send,recv,0
    def take(self):
        i=self.n; self.n+=1
        return self.s.at[i],self.r.at[i]
def rcopy(src,dst,sems,dev):
    a,b=sems.take()
    return pltpu.make_async_remote_copy(src_ref=src,dst_ref=dst,send_sem=a,recv_sem=b,device_id=dev,device_id_type=MESH)
class Gather:
    def __init__(self,pc,src,dst,rows,order,sems):
        self.pc,self.src,self.dst,self.rows,self.order,self.sems=pc,src,dst,rows,order,sems
        self.full=set(); self.pend=[]; self.core=[]
    def at(self,ref,over,full):
        pc=self.pc; ix={}
        for d in 'yzx':
            if d in over: ix[d]=over[d]
            elif d in full: ix[d]=slice(None)
            else: ix[d]=pl.ds(getattr(pc,d),1)
        i=(ix['y'],pl.ds(pc.c,1),ix['z'],ix['x'])
        if self.rows is not None: i=i+(pl.ds(*self.rows),)
        return ref.at[i]
    def to_core(self,over,full):
        sl=self.at(self.dst,over,full)
        k=rcopy(sl,sl,self.sems,self.pc.peer('c')); k.start(); self.core.append(k)
    def phase(self,p):
        if p>0: self.finish()
        if p==0: self.to_core({},self.full)
        d=self.order[p];
        for j in ((1,2,3) if d=='z' else (1,)):
            sl=self.at(self.dst,{},self.full)
            k=rcopy(sl,sl,self.sems,self.pc.peer(d,j)); k.start()
            self.pend.append((k,{d:pl.ds(getattr(self.pc,d)^j,1)},set(self.full)))
        self.full.add(d)
    def finish(self):
        for k,over,full in self.pend:
            k.wait_recv(); self.to_core(over,full)
        self.done=getattr(self,'done',[])+[k for k,_,_ in self.pend]
        self.pend=[]
    def drain(self):
        for k in self.core: k.wait_recv()
        for k in self.core+self.done: k.wait_send()
def local(src,dst,sem):
    k=pltpu.make_async_copy(src,dst,sem); k.start(); return k
def exchange(pc,src,dst,sems):
    out=[]
    for j in (2,3,1):
        p=(pc.dp,pc.t^j)
        k=rcopy(src.at[pc.t^j],dst.at[pc.t],sems,p); k.start(); out.append(k)
    return out
N_AG=6*11+11+6
ORD=(('z','y','x'),('z','x','y'))
def ag_kernel(s_ref,h_ref,c_ref,b_ref,g_ref,xo_ref,co_ref,bo_ref,ss,rs,ls):
    pc=Place(); sems=Sems(ss,rs)
    own=(pc.y,pc.c,pc.z,pc.x)
    loc=[local(s_ref.at[g],g_ref.at[g].at[own],ls.at[g]) for g in range(3)]
    loc+=[local(b_ref,bo_ref.at[own],ls.at[3]),local(h_ref.at[pc.t],xo_ref.at[pc.t],ls.at[4]),local(c_ref.at[pc.t],co_ref.at[pc.t],ls.at[5])]
    barrier(pc.peers_all())
    hx=exchange(pc,h_ref,xo_ref,sems)
    for k in loc: k.wait()
    gs=[Gather(pc,None,bo_ref,None,ORD[0],sems)]
    gs+=[Gather(pc,None,g_ref.at[g],(48*i,48),ORD[i],sems) for g in range(3) for i in range(2)]
    for p in range(3):
        for k in gs: k.phase(p)
    cx=exchange(pc,c_ref,co_ref,sems)
    for k in gs: k.finish()
    for k in gs: k.drain()
    for k in hx+cx: k.wait()
HBM=pl.BlockSpec(memory_space=pltpu.HBM); VM=pl.BlockSpec(memory_space=pltpu.VMEM)
def gather_all(s,h,c,b):
    return pl.pallas_call(ag_kernel,out_shape=[jax.ShapeDtypeStruct((3,2,2,4,2)+s.shape[1:],bf16),jax.ShapeDtypeStruct(h.shape,bf16),jax.ShapeDtypeStruct(c.shape,bf16),jax.ShapeDtypeStruct((2,2,4,2)+b.shape,f32)],
      in_specs=[HBM]*4,out_specs=[HBM]*4,scratch_shapes=[pltpu.SemaphoreType.DMA((N_AG,)),pltpu.SemaphoreType.DMA((N_AG,)),pltpu.SemaphoreType.DMA((6,))],
      compiler_params=pltpu.CompilerParams(collective_id=0,has_side_effects=True))(s,h,c,b)
N_RS=36+6+6
def rs_kernel(d_ref,v_ref,o_ref,x_ref,gs_ref,vs_ref,oo_ref,xo_ref,lc,rc,r1a,r1b,r2,r3,vb,vr,ss,rs,ls):
    pc=Place(); sems=Sems(ss,rs)
    loc=[local(o_ref.at[pc.t],oo_ref.at[pc.t],ls.at[0]),local(x_ref.at[pc.t],xo_ref.at[pc.t],ls.at[1])]
    lk=[]
    for k in range(6):
        g,i=divmod(k,2)
        lk.append(local(d_ref.at[g,:,pc.c,:,:,pl.ds(48*i,48)],lc.at[k],ls.at[2+k]))
    barrier(pc.peers_all())
    tail=[]
    cur=[]
    for k in range(6):
        g,i=divmod(k,2)
        q=rcopy(d_ref.at[g,:,1-pc.c,:,:,pl.ds(48*i,48)],rc.at[k],sems,pc.peer('c')); q.start(); cur.append(q)
    vb[0]=v_ref[...]
    vq=rcopy(vb.at[0],vr.at[0],sems,pc.peer('c')); vq.start()
    ox=exchange(pc,o_ref,oo_ref,sems)
    n1=[]
    for k in range(6):
        i=k%2
        lk[k].wait(); cur[k].wait_recv()
        def add(j,_):
            y,z,x=j//8,(j//2)%4,j%2
            lc[k,y,z,x]=(lc[k,y,z,x].astype(f32)+rc[k,y,z,x].astype(f32)).astype(bf16)
            return 0
        lax.fori_loop(0,16,add,0)
        if i==0:
            q=rcopy(lc.at[k,:,:,1-pc.x],r1a.at[k//2],sems,pc.peer('x'))
        else:
            q=rcopy(lc.at[k,1-pc.y],r1b.at[k//2],sems,pc.peer('y'))
        q.start(); n1.append(q)
    xx=exchange(pc,x_ref,xo_ref,sems)
    vq.wait_recv(); tail.append(vq)
    vb[1]=vb[0]+vr[0]
    vq=rcopy(vb.at[1],vr.at[1],sems,pc.peer('x')); vq.start()
    n2=[]
    for k in range(6):
        i=k%2
        n1[k].wait_recv()
        def add(j,_):
            if i==0:
                a,z=j//4,j%4
                lc[k,a,z,pc.x]=(lc[k,a,z,pc.x].astype(f32)+r1a[k//2,a,z].astype(f32)).astype(bf16)
            else:
                z,x=j//2,j%2
                lc[k,pc.y,z,x]=(lc[k,pc.y,z,x].astype(f32)+r1b[k//2,z,x].astype(f32)).astype(bf16)
            return 0
        lax.fori_loop(0,8,add,0)
        if i==0: q=rcopy(lc.at[k,1-pc.y,:,pc.x],r2.at[k],sems,pc.peer('y'))
        else: q=rcopy(lc.at[k,pc.y,:,1-pc.x],r2.at[k],sems,pc.peer('x'))
        q.start(); n2.append(q)
    vq.wait_recv(); tail.append(vq)
    vb[2]=vb[1]+vr[1]
    vq=rcopy(vb.at[2],vr.at[2],sems,pc.peer('y')); vq.start()
    n3=[]
    for k in range(6):
        n2[k].wait_recv()
        def add(z,_):
            lc[k,pc.y,z,pc.x]=(lc[k,pc.y,z,pc.x].astype(f32)+r2[k,z].astype(f32)).astype(bf16)
            return 0
        lax.fori_loop(0,4,add,0)
        qs=[]
        for j in (3,2,1):
            q=rcopy(lc.at[k,pc.y,pc.z^j,pc.x],r3.at[k,j-1],sems,pc.peer('z',j)); q.start(); qs.append(q)
        n3.append(qs)
    vq.wait_recv(); tail.append(vq)
    vb[3]=vb[2]+vr[2]
    vqs=[]
    for j in (3,2,1):
        q=rcopy(vb.at[3],vr.at[2+j],sems,pc.peer('z',j)); q.start(); vqs.append(q)
    for k in range(6):
        g,i=divmod(k,2)
        for q in n3[k]: q.wait_recv()
        gs_ref[g,48*i:48*i+48]=(lc[k,pc.y,pc.z,pc.x].astype(f32)+r3[k,0].astype(f32))+(r3[k,1].astype(f32)+r3[k,2].astype(f32))
    for q in vqs: q.wait_recv()
    vs_ref[...]=(vb[3]+vr[3])+(vr[4]+vr[5])
    for q in loc: q.wait()
    for q in ox+xx: q.wait()
    for q in cur+n1+n2+sum(n3,[])+vqs+tail: q.wait_send()
def reduce_all(d,v,o,x):
    r=d.shape[5]
    return pl.pallas_call(rs_kernel,out_shape=[jax.ShapeDtypeStruct((3,r,768),f32),jax.ShapeDtypeStruct(v.shape,f32),jax.ShapeDtypeStruct(o.shape,bf16),jax.ShapeDtypeStruct(x.shape,bf16)],
      in_specs=[HBM,VM,HBM,HBM],out_specs=[VM,VM,HBM,HBM],
      scratch_shapes=[pltpu.VMEM((6,2,4,2,48,768),bf16),pltpu.VMEM((6,2,4,2,48,768),bf16),pltpu.VMEM((3,2,4,48,768),bf16),pltpu.VMEM((3,4,2,48,768),bf16),pltpu.VMEM((6,4,48,768),bf16),pltpu.VMEM((6,3,48,768),bf16),pltpu.VMEM((4,16,768),f32),pltpu.VMEM((6,16,768),f32),
        pltpu.SemaphoreType.DMA((N_RS,)),pltpu.SemaphoreType.DMA((N_RS,)),pltpu.SemaphoreType.DMA((8,))],
      compiler_params=pltpu.CompilerParams(collective_id=1,has_side_effects=True,vmem_limit_bytes=62<<20))(d,v,o,x)


EPSILON = 1e-12


def norm_stats(r):
    center = r - jnp.mean(r, axis=-1, keepdims=True)
    inv = lax.rsqrt(jnp.mean(center * center, axis=-1, keepdims=True) + EPSILON)
    return center * inv, inv


def norm_back(cot, gain, xhat, inv):
    e = cot * gain
    grad = (e - jnp.mean(e, -1, keepdims=True) - xhat * jnp.mean(e * xhat, -1, keepdims=True)) * inv
    return grad, jnp.sum(cot * xhat, 0), jnp.sum(cot, 0)


def middle(x, cot, heads, w1, w2, w3, bias_o, bias_h, bias_d, shift1, shift2, gain1, gain2):
    ein = functools.partial(jnp.einsum, preferred_element_type=f32)
    hid = x.astype(f32)
    resid1 = hid + ein("tpw,tdw->pd", heads, w1[:, :, 512:]) + bias_o
    xhat1, inv1 = norm_stats(resid1)
    normed = xhat1 * gain1 + shift1
    low = normed.astype(bf16)
    pre = ein("pd,tdf->tpf", low, w2) + bias_h[:, None, :]
    act, gelu_back = jax.vjp(lambda v: jax.nn.gelu(v, approximate=False), pre)
    act = act.astype(bf16)
    resid2 = normed + ein("tpf,tdf->pd", act, w3) + bias_d
    xhat2, inv2 = norm_stats(resid2)
    out = (xhat2 * gain2 + shift2).astype(bf16)
    g2, dgain2, dshift2 = norm_back(cot.astype(f32), gain2, xhat2, inv2)
    g2low = g2.astype(bf16)
    d3 = ein("pd,tpf->tdf", g2low, act).astype(bf16)
    gpre = gelu_back(ein("pd,tdf->tpf", g2low, w3))[0].astype(bf16)
    d2 = ein("pd,tpf->tdf", low, gpre).astype(bf16)
    gn = g2 + ein("tpf,tdf->pd", gpre, w2)
    g1, dgain1, dshift1 = norm_back(gn, gain1, xhat1, inv1)
    g1low = g1.astype(bf16)
    dout = ein("pd,tpw->tdw", g1low, heads[:, :, 64:]).astype(bf16)
    dbh = jnp.sum(gpre, 1, dtype=f32)
    return out, g1, g1low, dout, d2, d3, (dgain1, dgain2, dshift1, dshift2, jnp.sum(g1, 0), dbh, jnp.sum(g2, 0))


def on_device(hidden_in, cotangent, prefix, w_qkv, w_out, w_in, w_down, biases, gains):
    rows = w_qkv.shape[0]
    n_t = lax.axis_size("tensor")
    t_me, d_me = lax.axis_index("tensor"), lax.axis_index("dp")
    n_dev = n_t * lax.axis_size("dp")
    s = jnp.stack([jnp.concatenate([w_qkv.reshape(rows, -1), w_out.T], axis=1), w_in, w_down.T])
    vecs = jnp.concatenate([biases, gains], 0)
    width = vecs.shape[1]
    vecs = jnp.pad(vecs, ((0, 4), (0, 128 - width)))
    seqs = lambda a: jnp.transpose(a, (1, 0, 2))
    h, c = seqs(hidden_in), seqs(cotangent)
    if lax.axis_size("dp") == 8:
        g, xs, cs, b = gather_all(s, h, c, vecs)
        b = b.transpose(2, 3, 0, 1, 4, 5)
    else:
        g = lax.all_gather(lax.all_gather(s, "dp", axis=1, tiled=True), "tensor", axis=1)
        xs = lax.all_to_all(h, "tensor", 0, 0, tiled=True)
        cs = lax.all_to_all(c, "tensor", 0, 0, tiled=True)
        b = lax.all_gather(vecs, ("dp", "tensor"), axis=0)
    w1, w2, w3 = [a.reshape(n_t, 768, 768) for a in g]
    vec = b.reshape(n_dev, 16, 128)[:, :12, :width].transpose(1, 0, 2).reshape(12, 768)
    x = xs.reshape(1024, 768)
    bqkv = jnp.pad(jnp.stack([vec[0].reshape(4, 192), jnp.zeros((4, 192), f32), vec[1].reshape(4, 192)], 1).reshape(4, 1, 576), ((0, 0), (0, 0), (0, 64)))
    my_prefix = lax.dynamic_slice_in_dim(prefix, t_me, 1, 0)
    proj, projT, heads, ot, lse = attn_fwd(my_prefix, x, w1, bqkv)
    out, g1, g1low, dout, d2, d3, small = middle(
        x, cs.reshape(1024, 768), heads, w1, w2, w3, vec[2], vec[3:7].reshape(4, 768), vec[7], vec[8], vec[9], vec[10], vec[11]
    )
    gproj = attn_bwd(my_prefix, g1low, w1, proj, projT, ot, lse)
    ein = functools.partial(jnp.einsum, preferred_element_type=f32)
    gp = gproj[:, :, :576]
    dqkv = ein("pd,tpc->tdc", x, gp).astype(bf16)
    dx = (g1 + ein("tpc,tdc->pd", gp, w1[:, :, :576])).astype(bf16)
    dgain1, dgain2, dshift1, dshift2, dbo, dbh, dbd = small
    dbq = jnp.sum(gp[:, :, :192], 1, dtype=f32).reshape(768)
    dbv = jnp.sum(gp[:, :, 384:], 1, dtype=f32).reshape(768)
    v = jnp.concatenate([jnp.stack([dbq, dbv, dbo]), dbh, jnp.stack([dbd, dshift1, dshift2, dgain1, dgain2]), jnp.zeros((4, 768), f32)])
    d = jnp.stack([jnp.concatenate([dqkv, dout], 2), d2, d3])
    o4, x4 = out.reshape(4, 256, 768), dx.reshape(4, 256, 768)
    if lax.axis_size("dp") == 8:
        gs, vs, oo, xx = reduce_all(d.reshape(3, 2, 2, 4, 2, rows, 768), v, o4, x4)
    else:
        part = lax.all_to_all(d, "tensor", 1, 1, tiled=True).astype(f32).sum(1)
        part = part.astype(bf16).reshape(3, -1, rows, 768)
        gs = lax.all_to_all(part, "dp", 1, 1, tiled=True).astype(f32).sum(1)
        vs = lax.psum(v, ("dp", "tensor"))
        oo = lax.all_to_all(o4, "tensor", 0, 0, tiled=True)
        xx = lax.all_to_all(x4, "tensor", 0, 0, tiled=True)
    mine = lax.dynamic_slice_in_dim(vs, (d_me * n_t + t_me) * width, width, 1)
    return (
        seqs(oo),
        seqs(xx),
        gs[0, :, :576].reshape(rows, 3, 192),
        gs[0, :, 576:].T,
        gs[1],
        gs[2].T,
        mine[:10],
        mine[10:12],
    )


def solution(mesh):
    placed = (
        P("tensor", "dp", None),
        P("tensor", "dp", None),
        P("dp"),
        P("dp", None, "tensor"),
        P("tensor", "dp"),
        P("dp", "tensor"),
        P("tensor", "dp"),
        P(None, ("dp", "tensor")),
        P(None, ("dp", "tensor")),
    )
    return jax.shard_map(on_device, mesh=mesh, in_specs=placed, out_specs=placed[:2] + placed[3:], check_vma=False)
```

time: 1480 us -> 536 us (0.36)
  waiting for transfers between devices: 555 us -> 0 us
  Pallas kernels: 0 us -> 338 us
  matrix products: 420 us -> 117 us
  blocking collectives: 261 us -> 0 us
  other arithmetic: 121 us -> 24.9 us
  local copies, waits for them, and re-layouts: 78.7 us -> 45.9 us
  starting transfers between devices: 26.4 us -> 0 us
    pallas_call x0 -> x4, Pallas kernels: none -> 338 us  [the longest x1 140 us: gather_all(): pl.pallas_call(ag_kernel, out_shape=[jax.ShapeDtypeStruct((3, 2, 2, 4, 2)...]
    dot_general x48 -> x10, matrix products: 420 us -> 117 us  [the longest x1 38.6 us: middle(): pre = ein('pd,tdf->tpf', low, w2) + bias_h[:, None, :]]
    all_gather x12 -> x0, waiting for transfers between devices: 268 us -> none  [the longest x2 74.2 us: fetch_weights(): lax.all_gather(w_in, 'dp', axis=0, tiled=True)]
    all_gather x6 -> x0, blocking collectives: 223 us -> none  [the longest x2 75.1 us: fetch_weights(): lax.all_gather(w_qkv, 'dp', axis=0, tiled=True)]
    reduce_scatter x8 -> x0, waiting for transfers between devices: 211 us -> none  [the longest x2 75.3 us: micro_step(): lax.psum_scatter(jnp.einsum('psf,df->psd', row_block, mat_in, preferred_e...]
    all_to_all x4 -> x0, waiting for transfers between devices: 73.2 us -> none  [sent_and_summed(): lax.all_to_all(blocks, axis, split_axis=0, concat_axis=0, tiled=True)]
    reduce_sum x28 -> x7, other arithmetic: 52.1 us -> 8.85 us  [the longest x2 4.73 us: norm_back(): return (grad, jnp.sum(cot * xhat, 0), jnp.sum(cot, 0))]
    convert_element_type x8 -> x1, other arithmetic: 41.3 us -> 0.16 us  [middle(): g1low = g1.astype(bf16)]
  transfers between devices with their start and end apart: 24 -> 0, of which waited for: 18 -> 0; matrix products, arithmetic and copies ran while one was open for 21% -> 0% of each run, Pallas kernels for 0% -> 0%
where the time goes in v1:
time: 536 us; the launch traced here: 528 us
  Pallas kernels  338 us (63%)
  matrix products  117 us (22%)
  local copies, waits for them, and re-layouts  45.9 us (9%)
  other arithmetic  24.9 us (5%)
    pallas_call x1, Pallas kernels, gather_all(): pl.pallas_call(ag_kernel, out_shape=[jax.ShapeDtypeStruct((3, 2, 2, 4, 2)...  140 us
    pallas_call x1, Pallas kernels, reduce_all(): pl.pallas_call(rs_kernel, out_shape=[jax.ShapeDtypeStruct((3, r, 768), f3...  130 us
    dot_general x1, matrix products, middle(): pre = ein('pd,tdf->tpf', low, w2) + bias_h[:, None, :]  38.6 us
    pallas_call x1, Pallas kernels, attn_bwd(): pl.pallas_call(functools.partial(bwd_kernel), grid_spec=pltpu.PrefetchSca...  35.9 us
    pallas_call x1, Pallas kernels, attn_fwd(): pl.pallas_call(fwd_kernel, grid_spec=pltpu.PrefetchScalarGridSpec(num_sca...  31.8 us
    dot_general x1, matrix products, middle(): gpre = gelu_back(ein('pd,tdf->tpf', g2low, w3))[0].astype(bf16)  18.3 us
    unnamed x43, local copies, waits for them, and re-layouts  14.5 us
    another operation x1, local copies, waits for them, and re-layouts, on_device(): w1, w2, w3 = [a.reshape(n_t, 768, 768) for a in g]  11.8 us

profile of v1, /device:TPU:0, one launch (start us, length us, event | category | flops | bytes accessed | tf_op | source)
XLA Modules:
  0.0 527.8 jit_solution(17415987556120681987)
XLA Ops:
  0.7 0.9 copy.39
  1.6 1.1 copy.38
  2.6 0.2 copy.40
  2.8 0.1 maximum_bitcast_fusion
  2.9 1.8 pad_maximum_fusion.2.s_ref
  4.7 4.0 copy_bitcast_fusion
  8.6 0.6 select_maximum_fusion.b_ref
  9.3 139.9 %shard_map.152 = (bf16[3,2,2,4,2,96,768]{6,5,4,3,2,1,0:T(8,128)(2,1)}, bf16[4,256,768]{2,1,0:T(8,128)(2,1)}, bf16[4,256,768]{2,1,0:T(8,128)(2,1)}, f32[2,2,4,2,16,128]{5,4,3,2,1,0:T(8,128)}) custom-call(bf16[3,96,768]{2,1,0:T(8,128)(2,1)} %pad_maximum_fusion.2.s_ref, bf16[4,256,768]{2,1,0:T(8,128)(2,1)} %get-tuple-element.89.h_ref, ...), custom_call_target="tpu_custom_call" | custom-call | tf_op jit(solution)/shard_map/pallas_call | solution.py:188
  149.1 1.0 copy.43
  150.2 0.1 add.101
  150.3 0.0 copy-start.12
  150.3 11.8 %fusion.70 = (bf16[1,2,2,4,2,96,768]{6,5,4,3,2,1,0:T(8,128)(2,1)}, bf16[1,2,2,4,2,96,768]{6,5,4,3,2,1,0:T(8,128)(2,1)}, bf16[1,2,2,4,2,96,768]{6,5,4,3,2,1,0:T(8,128)(2,1)}) fusion(bf16[3,2,2,4,2,96,768]{6,5,4,3,2,1,0:T(8,128)(2,1)} %get-tuple-element.24), kind=kLoop, calls=%fused_computation.116 | loop fusion | bytes 28311552 | tf_op jit(solution)/shard_map/unstack | solution.py:339
  162.0 0.4 slice_reduce_fusion
  162.4 0.1 add.94
  162.5 0.6 dynamic_slice.6.prefix_ref
  163.1 0.1 stack_reshape_squeeze.7
  163.2 0.1 stack_reshape_squeeze.6
  163.2 0.1 pad.16.clone
  163.3 0.1 pad_maximum_fusion.3
  163.4 0.1 reshape.132
  163.5 0.6 pad.9.b_ref
  164.1 31.8 %shard_map.153 = (bf16[4,1024,640]{2,1,0:T(8,128)(2,1)}, bf16[4,640,1024]{2,1,0:T(8,128)(2,1)}, bf16[4,1024,256]{2,1,0:T(8,128)(2,1)}, bf16[4,256,1024]{2,1,0:T(8,128)(2,1)}, f32[4,8,1024]{2,1,0:T(8,128)}) custom-call(s32[1]{0:T(128)} %dynamic_slice.6.prefix_ref, bf16[1024,768]{1,0:T(8,128)(2,1)} %bitcast.211, bf16[4,768,768]{2,1,0:T(8,128)(2,1)} %bitcast.194, ...), custom_call_target="tpu_custom_call" | custom-call | tf_op jit(solution)/shard_map/pallas_call | solution.py:55
  195.9 4.5 fusion.71
  200.4 0.1 add.98
  200.5 0.1 mul.149
  200.6 0.5 multiply_reduce_fusion.3
  201.1 38.6 %fusion.9 = (bf16[4,1024,768]{1,2,0:T(8,128)(2,1)}, f32[4,1024,768]{1,2,0:T(8,128)}, f32[4,768,1024]{2,1,0:T(8,128)}) fusion(f32[4,768]{1,0:T(4,128)S(1)} %add.101, bf16[4,768,768]{2,1,0:T(8,128)(2,1)} %bitcast.202, f32[1024,768]{1,0:T(8,128)S(1)} %get-tuple-element.81, f32[768]{0:T(1024)S(1)} %add.98, f32[768]{0:T(1024)S(1)} %mul.149, ...), kind=kOutput, calls=%fused_computation.18 | convolution fusion | flops 5043388416 | bytes 39348224 | tf_op jit(solution)/shard_map/pd,tdf->tpf/dot_general | solution.py:301
  239.6 0.1 add.105
  239.7 10.3 %fusion.72 = (f32[1024]{0:T(1024)S(1)}, f32[1024,768]{1,0:T(8,128)S(1)}) fusion(f32[768]{0:T(1024)S(1)} %add.105, bf16[4,1024,768]{1,2,0:T(8,128)(2,1)} %get-tuple-element.72, bf16[4,768,768]{2,1,0:T(8,128)(2,1)} %bitcast.204, f32[768]{0:T(1024)S(1)} %add.98, f32[768]{0:T(1024)S(1)} %mul.149, f32[1024]{0:T(1024)S(1)} %add_rsqrt_fusion.1, ...), kind=kOutput, calls=%fused_computation.118 | convolution fusion | flops 4837342208 | bytes 17323008 | tf_op jit(solution)/shard_map/tpf,tdf->pd/dot_general | solution.py:304
  250.0 0.5 multiply_reduce_fusion.2
  250.5 0.1 mul.141
  250.6 0.1 add.110
  250.7 4.0 fusion.36
  254.7 0.8 convert_reduce_fusion.3
  255.5 1.2 fusion.66
  256.8 6.9 %convolution_convert_fusion = bf16[4,768,768]{1,2,0:T(8,128)(2,1)} fusion(bf16[4,1024,768]{1,2,0:T(8,128)(2,1)S(1)} %bitcast.223, f32[1024,768]{1,0:T(8,128)S(1)} %get-tuple-element.69), kind=kOutput, calls=%fused_computation.69 | convolution fusion | flops 4834983936 | bytes 14155776 | tf_op jit(solution)/shard_map/pd,tpf->tdf/dot_general | solution.py:309
  263.7 18.3 %convert_reduce_fusion = (f32[4,768]{1,0:T(4,128)S(1)}, bf16[4,1024,768]{1,2,0:T(8,128)(2,1)}) fusion(f32[4,1024,768]{1,2,0:T(8,128)} %get-tuple-element.73, bf16[4,768,768]{2,1,0:T(8,128)(2,1)} %bitcast.205, f32[1024,768]{1,0:T(8,128)} %copy-done.5, f32[4,768,1024]{2,1,0:T(8,128)} %get-tuple-element.82, f32[4,768]{1,0:T(4,128)S(1)} %add.101), kind=kOutput, calls=%fused_computation.19 | convolution fusion | flops 4886098944 | bytes 39346176 | tf_op jit(solution)/shard_map/pd,tdf->tpf/dot_general | solution.py:310
  282.0 10.2 %convolution_convert_fusion.1 = bf16[4,768,768]{1,2,0:T(8,128)(2,1)} fusion(bf16[4,1024,768]{1,2,0:T(8,128)(2,1)} %get-tuple-element.87, f32[1024,768]{1,0:T(8,128)S(1)} %copy-done.2, f32[768]{0:T(1024)S(1)} %add.98, f32[768]{0:T(1024)S(1)} %mul.149, f32[1024]{0:T(1024)S(1)} %add_rsqrt_fusion.1, f32[1024]{0:T(1024)S(1)} %broadcast_multiply_fusion.4), kind=kOutput, calls=%fused_computation.70 | convolution fusion | flops 4838129664 | bytes 14170112 | tf_op jit(solution)/shard_map/pd,tpf->tdf/dot_general | solution.py:311
  292.2 8.8 %multiply_reduce_fusion = (f32[768]{0:T(1024)S(1)}, f32[1024]{0:T(1024)S(1)}, f32[1024]{0:T(1024)S(1)}, f32[768]{0:T(1024)S(1)}, f32[1024,768]{1,0:T(8,128)S(1)}) fusion(f32[1024,768]{1,0:T(8,128)S(1)} %copy-done.2, f32[1024]{0:T(1024)S(1)} %add_rsqrt_fusion.1, f32[1024]{0:T(1024)S(1)} %broadcast_multiply_fusion.4, f32[768]{0:T(1024)S(1)} %mul.149, ...), kind=kOutput, calls=%fused_computation.61 | convolution fusion | flops 4839698432 | bytes 20472832 | tf_op jit(solution)/shard_map/tpf,tdf->pd/dot_general | solution.py:312
  301.0 1.2 fusion.68
  302.3 0.2 convert_element_type.79.g_ref
  302.4 2.6 copy-done.11
  305.0 3.0 fusion.56
  307.9 35.9 %shard_map.154 = bf16[4,1024,640]{2,1,0:T(8,128)(2,1)} custom-call(s32[1]{0:T(128)} %dynamic_slice.6.prefix_ref, bf16[1024,768]{1,0:T(8,128)(2,1)} %copy-done.4, bf16[4,768,768]{2,1,0:T(8,128)(2,1)} %bitcast.196, bf16[4,1024,640]{2,1,0:T(8,128)(2,1)} %get-tuple-element.26.proj_ref, bf16[4,640,1024]{2,1,0:T(8,128)(2,1)} %get-tuple-element.27.projT_ref, ...), custom_call_target="tpu_custom_call" | custom-call | tf_op jit(solution)/shard_map/pallas_call | solution.py:99
  343.9 7.0 %convert_bitcast_fusion = bf16[4,768,576]{1,2,0:T(8,128)(2,1)S(1)} fusion(bf16[1024,768,1]{1,0,2:T(8,128)(2,1)} %bitcast.213, bf16[4,1024,640]{2,1,0:T(8,128)(2,1)} %shard_map.154), kind=kOutput, calls=%fused_computation.41 | convolution fusion | flops 3625648128 | bytes 10354688 | tf_op jit(solution)/shard_map/pd,tpc->tdc/dot_general | solution.py:351
  351.0 2.4 pad_maximum_fusion.1
  353.4 6.8 %copy.53 = bf16[4,768,768]{2,1,0:T(8,128)(2,1)} copy(bf16[4,768,768]{1,2,0:T(8,128)(2,1)} %pad_maximum_fusion.1) | data formatting | bytes 9437184 | tf_op jit(solution)/shard_map/concatenate | solution.py:357
  360.2 10.9 %pad_maximum_fusion.d_ref = bf16[3,2,2,4,2,96,768]{6,5,4,3,2,1,0:T(8,128)(2,1)} fusion(bf16[1,2,2,4,2,96,768]{6,5,4,3,2,1,0:T(8,128)(2,1)} %bitcast.206, bf16[1,2,2,4,2,96,768]{6,5,4,3,2,1,0:T(8,128)(2,1)} %bitcast.207, bf16[1,2,2,4,2,96,768]{6,5,4,3,2,1,0:T(8,128)(2,1)} %bitcast.198), kind=kLoop, calls=%fused_computation.1 | loop fusion | flops 14155776 | bytes 28311552 | tf_op jit(solution)/shard_map/stack | solution.py:357
  371.1 0.6 slice-done.1
  371.8 0.7 convert_reduce_fusion.1
  372.5 0.1 stack_reshape.6
  372.5 0.1 stack_reshape.7
  372.7 1.3 concatenate.16.v_ref
  374.0 10.0 %fusion.27 = bf16[1024,768]{1,0:T(8,128)(2,1)} fusion(f32[1024,768]{1,0:T(8,128)} %copy-done.3, bf16[4,768,768]{2,1,0:T(8,128)(2,1)} %bitcast.197, bf16[4,1024,640]{2,1,0:T(8,128)(2,1)} %shard_map.154), kind=kOutput, calls=%fused_computation.43 | convolution fusion | flops 3625451520 | bytes 13893632 | tf_op jit(solution)/shard_map/tpc,tdc->pd/dot_general | solution.py:352
  383.9 130.3 %shard_map.155 = (f32[3,96,768]{2,1,0:T(8,128)}, f32[16,768]{1,0:T(8,128)}, bf16[4,256,768]{2,1,0:T(8,128)(2,1)}, bf16[4,256,768]{2,1,0:T(8,128)(2,1)}) custom-call(bf16[3,2,2,4,2,96,768]{6,5,4,3,2,1,0:T(8,128)(2,1)} %pad_maximum_fusion.d_ref, f32[16,768]{1,0:T(8,128)} %concatenate.16.v_ref, bf16[4,256,768]{2,1,0:T(8,128)(2,1)} %bitcast.201, ...), custom_call_target="tpu_custom_call" | custom-call | tf_op jit(solution)/shard_map/pallas_call | solution.py:272
  514.3 3.8 copy.61
  518.2 3.8 copy.62
  521.9 0.1 copy.60
  522.1 0.9 copy.63
  523.0 0.1 slice_bitcast_fusion.3
  523.1 0.7 copy.64
  523.8 0.8 slice_bitcast_fusion
  524.7 1.4 constant_dynamic-slice_fusion
  526.0 1.3 dynamic-slice.1
  (56 shorter events, 0.2 us)
Async XLA Ops:
  0.6 8.0 %copy-start.10 = (f32[2,24]{1,0:T(2,128)S(1)}, f32[2,24]{1,0:T(2,128)}, u32[]{:S(2)}) copy-start(f32[2,24]{1,0:T(2,128)} %param.17) | copy-start | bytes 580
  0.6 8.0 %copy-start.9 = (f32[10,24]{1,0:T(8,128)S(1)}, f32[10,24]{1,0:T(8,128)}, u32[]{:S(2)}) copy-start(f32[10,24]{1,0:T(8,128)} %param.16) | copy-start | bytes 2884
  150.3 12.2 %copy-start.12 = (s32[4]{0:T(128)S(1)}, s32[4]{0:T(128)}, u32[]{:S(2)}) copy-start(s32[4]{0:T(128)} %param.11) | copy-start | bytes 52
  200.4 39.3 %copy-start.1 = (f32[1024,768]{1,0:T(8,128)}, f32[1024,768]{1,0:T(8,128)S(1)}, u32[]{:S(2)}) copy-start(f32[1024,768]{1,0:T(8,128)S(1)} %get-tuple-element.81) | copy-start | bytes 9437188
  250.7 4.0 copy-start
  250.7 6.0 %slice-start.2 = ((s8[6291456]{0:T(1024)(128)(4,1)}), s8[4194304]{0:T(1024)(128)(4,1)S(1)}, s32[]{:S(2)}) async-start(s8[6291456]{0:T(1024)(128)(4,1)} %bitcast.222), calls=%async_computation.2 | async-start | bytes 8388608
  254.7 2.1 slice-start.3
  256.7 6.9 %copy-start.5 = (f32[1024,768]{1,0:T(8,128)}, f32[1024,768]{1,0:T(8,128)S(1)}, u32[]{:S(2)}) copy-start(f32[1024,768]{1,0:T(8,128)S(1)} %get-tuple-element.69) | copy-start | bytes 9437188
  263.7 18.3 %copy-start.2 = (f32[1024,768]{1,0:T(8,128)S(1)}, f32[1024,768]{1,0:T(8,128)}, u32[]{:S(2)}) copy-start(f32[1024,768]{1,0:T(8,128)} %copy-done.1) | copy-start | bytes 9437188
  282.0 10.2 %copy-start.6 = (f32[1024,768]{1,0:T(8,128)S(1)}, f32[1024,768]{1,0:T(8,128)}, u32[]{:S(2)}) copy-start(f32[1024,768]{1,0:T(8,128)} %copy-done.5) | copy-start | bytes 9437188
  282.0 10.2 %copy-start.13 = (bf16[4,1024,768]{1,2,0:T(8,128)(2,1)S(1)}, bf16[4,1024,768]{1,2,0:T(8,128)(2,1)}, u32[]{:S(2)}) copy-start(bf16[4,1024,768]{1,2,0:T(8,128)(2,1)} %get-tuple-element.87) | copy-start | bytes 18874372
  302.2 5.7 %copy-start.3 = (f32[1024,768]{1,0:T(8,128)}, f32[1024,768]{1,0:T(8,128)S(1)}, u32[]{:S(2)}) copy-start(f32[1024,768]{1,0:T(8,128)S(1)} %get-tuple-element.71) | copy-start | bytes 9437188
  302.3 2.7 copy-start.11
  305.0 3.0 copy-start.4
  343.9 7.1 %copy-start.7 = (bf16[4,768,192]{1,2,0:T(8,128)(2,1)S(1)}, bf16[4,768,192]{1,2,0:T(8,128)(2,1)}, u32[]{:S(2)}) copy-start(bf16[4,768,192]{1,2,0:T(8,128)(2,1)} %fusion.56) | copy-start | bytes 3538948
  353.4 17.7 %slice-start = ((s8[5242880]{0:T(1024)(128)(4,1)}), s8[1048576]{0:T(1024)(128)(4,1)S(1)}, s32[]{:S(2)}) async-start(s8[5242880]{0:T(1024)(128)(4,1)} %bitcast.199), calls=%async_computation | async-start | bytes 2097152
  360.2 11.5 %slice-start.1 = ((s8[5242880]{0:T(1024)(128)(4,1)}), s8[4194304]{0:T(1024)(128)(4,1)S(1)}, s32[]{:S(2)}) async-start(s8[5242880]{0:T(1024)(128)(4,1)} %bitcast.199), calls=%async_computation.1 | async-start | bytes 8388608
  514.3 7.6 %copy-start.8 = (f32[3,96,768]{2,1,0:T(8,128)S(1)}, f32[3,96,768]{2,1,0:T(8,128)}, u32[]{:S(2)}) copy-start(f32[3,96,768]{2,1,0:T(8,128)} %get-tuple-element.32) | copy-start | bytes 2654212

commit v2 on v1

--- a/solution.py
+++ b/solution.py
@@ -188,92 +188,275 @@
     return pl.pallas_call(ag_kernel,out_shape=[jax.ShapeDtypeStruct((3,2,2,4,2)+s.shape[1:],bf16),jax.ShapeDtypeStruct(h.shape,bf16),jax.ShapeDtypeStruct(c.shape,bf16),jax.ShapeDtypeStruct((2,2,4,2)+b.shape,f32)],
       in_specs=[HBM]*4,out_specs=[HBM]*4,scratch_shapes=[pltpu.SemaphoreType.DMA((N_AG,)),pltpu.SemaphoreType.DMA((N_AG,)),pltpu.SemaphoreType.DMA((6,))],
       compiler_params=pltpu.CompilerParams(collective_id=0,has_side_effects=True))(s,h,c,b)
-N_RS=36+6+6
-def rs_kernel(d_ref,v_ref,o_ref,x_ref,gs_ref,vs_ref,oo_ref,xo_ref,lc,rc,r1a,r1b,r2,r3,vb,vr,ss,rs,ls):
-    pc=Place(); sems=Sems(ss,rs)
-    loc=[local(o_ref.at[pc.t],oo_ref.at[pc.t],ls.at[0]),local(x_ref.at[pc.t],xo_ref.at[pc.t],ls.at[1])]
-    lk=[]
-    for k in range(6):
-        g,i=divmod(k,2)
-        lk.append(local(d_ref.at[g,:,pc.c,:,:,pl.ds(48*i,48)],lc.at[k],ls.at[2+k]))
+def point(steps, k, h):
+    for kk in range(4):
+        todo = steps.get((kk, h))
+        if todo:
+            @pl.when(k == kk)
+            def _(todo=todo):
+                for step in todo:
+                    step()
+
+
+def add_into(dst, src, n, pick_dst, pick_src):
+    def body(j, _):
+        a, b = pick_dst(j), pick_src(j)
+        dst[a] = (dst[a].astype(f32) + src[b].astype(f32)).astype(bf16)
+        return 0
+    lax.fori_loop(0, n, body, 0)
+
+
+class Reduce:
+    def __init__(self, pc, d_ref, half, lc, rc, r1, r2, r3, sems, lsem):
+        self.pc, self.lc, self.rc, self.r1, self.r2, self.r3 = pc, lc, rc, r1, r2, r3
+        rows = pl.ds(48 * half, 48)
+        self.own = pltpu.make_async_copy(d_ref.at[:, pc.c, :, :, rows], lc, lsem)
+        self.q0 = rcopy(d_ref.at[:, 1 - pc.c, :, :, rows], rc, sems, pc.peer("c"))
+        self.q1 = rcopy(lc.at[:, :, 1 - pc.x], r1, sems, pc.peer("x"))
+        self.q2 = [rcopy(lc.at[:, pc.z ^ j, pc.x], r2.at[j - 1], sems, pc.peer("z", j)) for j in (3, 2, 1)]
+        self.q3 = rcopy(lc.at[1 - pc.y, pc.z, pc.x], r3, sems, pc.peer("y"))
+
+    def s0(self):
+        self.own.start()
+        self.q0.start()
+
+    def s1(self):
+        self.own.wait()
+        self.q0.wait_recv()
+        at = lambda j: (j // 8, (j // 2) % 4, j % 2)
+        add_into(self.lc, self.rc, 16, at, at)
+        self.q1.start()
+
+    def s2(self):
+        self.q1.wait_recv()
+        add_into(self.lc, self.r1, 8, lambda j: (j // 4, j % 4, self.pc.x), lambda j: (j // 4, j % 4))
+        for q in self.q2:
+            q.start()
+
+    def s3(self):
+        pc = self.pc
+        for q in self.q2:
+            q.wait_recv()
+        for y in range(2):
+            at = (y, pc.z, pc.x)
+            total = (self.lc[at].astype(f32) + self.r2[0, y].astype(f32)) + (self.r2[1, y].astype(f32) + self.r2[2, y].astype(f32))
+            self.lc[at] = total.astype(bf16)
+        self.q3.start()
+
+    def s4(self, out_ref, rows):
+        pc = self.pc
+        self.q3.wait_recv()
+        out_ref[rows] = self.lc[pc.y, pc.z, pc.x].astype(f32) + self.r3[...].astype(f32)
+
+    def end(self):
+        for q in [self.q0, self.q1, self.q3] + self.q2:
+            q.wait_send()
+
+
+N_C = 4 * 6 + 1 + 1 + 1 + 2 + 6 + 6 + 6
+
+
+def back_kernel(
+    prefix_ref, x_ref, g_ref, gf_ref, w_ref, proj_ref, projT_ref, ot_ref, lse_ref, dout_ref, d_ref, v_ref, out_ref,
+    gs_ref, vs_ref, oo_ref, xo_ref,
+    xT, gl, dxa, w_b, proj_b, projT_b, ot_b, lse_b, dout_b,
+    zq, zdo, qm, dom, pt, ds, mask_ref, gt, dqt, dkb, dvb, gproj,
+    lc, rc, r1, r2, r3, dwb, cr, yr, xr, zr, vb, vr, xst, ss, rs, ls, ins,
+):
+    pc = Place()
+    sems = Sems(ss, rs)
+    w1 = w_ref.at[0]
+    lane = lax.broadcasted_iota(jnp.int32, (1, 256), 1)
+
+    def loads(k, slot):
+        t = pc.t ^ (3 - k)
+        pairs = [
+            (w1.at[t // 2, t % 2], w_b), (proj_ref.at[t], proj_b), (projT_ref.at[t], projT_b),
+            (ot_ref.at[t], ot_b), (lse_ref.at[t], lse_b), (dout_ref.at[t], dout_b),
+        ]
+        return [pltpu.make_async_copy(a, b.at[slot], ins.at[slot, n]) for n, (a, b) in enumerate(pairs)]
+
+    first = loads(0, 0)
+    for q in first:
+        q.start()
+    l_x = local(x_ref, xst, ls.at[4])
+    l_g = local(g_ref, gl, ls.at[5])
+    l_f = local(gf_ref, dxa, ls.at[6])
     barrier(pc.peers_all())
-    tail=[]
-    cur=[]
-    for k in range(6):
-        g,i=divmod(k,2)
-        q=rcopy(d_ref.at[g,:,1-pc.c,:,:,pl.ds(48*i,48)],rc.at[k],sems,pc.peer('c')); q.start(); cur.append(q)
-    vb[0]=v_ref[...]
-    vq=rcopy(vb.at[0],vr.at[0],sems,pc.peer('c')); vq.start()
-    ox=exchange(pc,o_ref,oo_ref,sems)
-    n1=[]
-    for k in range(6):
-        i=k%2
-        lk[k].wait(); cur[k].wait_recv()
-        def add(j,_):
-            y,z,x=j//8,(j//2)%4,j%2
-            lc[k,y,z,x]=(lc[k,y,z,x].astype(f32)+rc[k,y,z,x].astype(f32)).astype(bf16)
-            return 0
-        lax.fori_loop(0,16,add,0)
-        if i==0:
-            q=rcopy(lc.at[k,:,:,1-pc.x],r1a.at[k//2],sems,pc.peer('x'))
-        else:
-            q=rcopy(lc.at[k,1-pc.y],r1b.at[k//2],sems,pc.peer('y'))
-        q.start(); n1.append(q)
-    xx=exchange(pc,x_ref,xo_ref,sems)
-    vq.wait_recv(); tail.append(vq)
-    vb[1]=vb[0]+vr[0]
-    vq=rcopy(vb.at[1],vr.at[1],sems,pc.peer('x')); vq.start()
-    n2=[]
-    for k in range(6):
-        i=k%2
-        n1[k].wait_recv()
-        def add(j,_):
-            if i==0:
-                a,z=j//4,j%4
-                lc[k,a,z,pc.x]=(lc[k,a,z,pc.x].astype(f32)+r1a[k//2,a,z].astype(f32)).astype(bf16)
-            else:
-                z,x=j//2,j%2
-                lc[k,pc.y,z,x]=(lc[k,pc.y,z,x].astype(f32)+r1b[k//2,z,x].astype(f32)).astype(bf16)
-            return 0
-        lax.fori_loop(0,8,add,0)
-        if i==0: q=rcopy(lc.at[k,1-pc.y,:,pc.x],r2.at[k],sems,pc.peer('y'))
-        else: q=rcopy(lc.at[k,pc.y,:,1-pc.x],r2.at[k],sems,pc.peer('x'))
-        q.start(); n2.append(q)
-    vq.wait_recv(); tail.append(vq)
-    vb[2]=vb[1]+vr[1]
-    vq=rcopy(vb.at[2],vr.at[2],sems,pc.peer('y')); vq.start()
-    n3=[]
-    for k in range(6):
-        n2[k].wait_recv()
-        def add(z,_):
-            lc[k,pc.y,z,pc.x]=(lc[k,pc.y,z,pc.x].astype(f32)+r2[k,z].astype(f32)).astype(bf16)
-            return 0
-        lax.fori_loop(0,4,add,0)
-        qs=[]
-        for j in (3,2,1):
-            q=rcopy(lc.at[k,pc.y,pc.z^j,pc.x],r3.at[k,j-1],sems,pc.peer('z',j)); q.start(); qs.append(q)
-        n3.append(qs)
-    vq.wait_recv(); tail.append(vq)
-    vb[3]=vb[2]+vr[2]
-    vqs=[]
-    for j in (3,2,1):
-        q=rcopy(vb.at[3],vr.at[2+j],sems,pc.peer('z',j)); q.start(); vqs.append(q)
-    for k in range(6):
-        g,i=divmod(k,2)
-        for q in n3[k]: q.wait_recv()
-        gs_ref[g,48*i:48*i+48]=(lc[k,pc.y,pc.z,pc.x].astype(f32)+r3[k,0].astype(f32))+(r3[k,1].astype(f32)+r3[k,2].astype(f32))
-    for q in vqs: q.wait_recv()
-    vs_ref[...]=(vb[3]+vr[3])+(vr[4]+vr[5])
-    for q in loc: q.wait()
-    for q in ox+xx: q.wait()
-    for q in cur+n1+n2+sum(n3,[])+vqs+tail: q.wait_send()
-def reduce_all(d,v,o,x):
-    r=d.shape[5]
-    return pl.pallas_call(rs_kernel,out_shape=[jax.ShapeDtypeStruct((3,r,768),f32),jax.ShapeDtypeStruct(v.shape,f32),jax.ShapeDtypeStruct(o.shape,bf16),jax.ShapeDtypeStruct(x.shape,bf16)],
-      in_specs=[HBM,VM,HBM,HBM],out_specs=[VM,VM,HBM,HBM],
-      scratch_shapes=[pltpu.VMEM((6,2,4,2,48,768),bf16),pltpu.VMEM((6,2,4,2,48,768),bf16),pltpu.VMEM((3,2,4,48,768),bf16),pltpu.VMEM((3,4,2,48,768),bf16),pltpu.VMEM((6,4,48,768),bf16),pltpu.VMEM((6,3,48,768),bf16),pltpu.VMEM((4,16,768),f32),pltpu.VMEM((6,16,768),f32),
-        pltpu.SemaphoreType.DMA((N_RS,)),pltpu.SemaphoreType.DMA((N_RS,)),pltpu.SemaphoreType.DMA((8,))],
-      compiler_params=pltpu.CompilerParams(collective_id=1,has_side_effects=True,vmem_limit_bytes=62<<20))(d,v,o,x)
+    red = {}
+    for n, (g, i) in enumerate(((1, 0), (1, 1), (0, 0), (0, 1))):
+        red[n] = Reduce(pc, d_ref.at[g], i, lc.at[n], rc.at[n], r1.at[n], r2.at[n], r3.at[n], sems, ls.at[n])
+        red[n].s0()
+    ox = exchange(pc, out_ref, oo_ref, sems)
+    l_o = [local(out_ref.at[pc.t], oo_ref.at[pc.t], ls.at[7])]
+    q_c0 = rcopy(dwb.at[0], cr.at[0], sems, pc.peer("c"))
+    q_y = rcopy(dwb.at[1], yr, sems, pc.peer("y"))
+    q_c1 = rcopy(dwb.at[2], cr.at[1], sems, pc.peer("c"))
+    half = [pl.ds(48 * i, 48) for i in range(2)]
+    q_x = [rcopy(dwb.at[3, :, 1 - pc.x, half[i]], xr.at[i], sems, pc.peer("x")) for i in range(2)]
+    q_z = [[rcopy(dwb.at[3, pc.z ^ j, pc.x, half[i]], zr.at[i, j - 1], sems, pc.peer("z", j)) for j in (3, 2, 1)] for i in range(2)]
+    steps = {
+        (0, 1): [red[0].s1], (0, 2): [red[1].s1], (0, 3): [red[2].s1], (1, 1): [red[3].s1],
+        (1, 3): [red[0].s2], (2, 3): [red[1].s2], (3, 0): [red[0].s3], (3, 3): [red[2].s2],
+    }
+    masks(mask_ref, prefix_ref[0])
+    zq[...] = jnp.zeros_like(zq)
+    zdo[...] = jnp.zeros_like(zdo)
+    gproj[:, 576:640] = jnp.zeros((L, 64), bf16)
+    vb[0] = v_ref[...]
+    l_x.wait()
+    xT[...] = xst[...].reshape(L, 768).T
+    l_g.wait()
+    l_f.wait()
+
+    def group(k, _):
+        slot = k % 2
+        for q in loads(k, slot):
+            q.wait()
+
+        @pl.when(k < 3)
+        def _():
+            for q in loads(k + 1, 1 - slot):
+                q.start()
+
+        t = pc.t ^ (3 - k)
+        w, pj, pjT, o_t, lse = w_b.at[slot], proj_b.at[slot], projT_b.at[slot], ot_b.at[slot], lse_b.at[slot]
+        gh = dotf(gl[...], w[...].reshape(768, 768)[:, 512:768]).astype(bf16)
+        gt[...] = gh.T
+        for h in range(3):
+            point(steps, k, h)
+            own = slice(64 + 64 * h, 128 + 64 * h)
+            zq[h, own, :] = pjT[64 * h : 64 * h + 64, :]
+            zdo[h, 64 * h : 64 * h + 64, :] = gt[own, :] * 0.125
+            qm[...] = jnp.where((lane >= 64 * h) & (lane < 64 * h + 64), pj[:, 0:256], 0)
+            dom[...] = jnp.where((lane >= 64 * h + 64) & (lane < 64 * h + 128), gh, 0)
+            d = jnp.sum(gt[own, :].astype(f32) * o_t[own, :].astype(f32), axis=0, keepdims=True) * 0.125
+            for qb in range(4):
+                nk = NK[qb]
+                qs = slice(qb * QB, qb * QB + QB)
+                st = masked(dotf(pj[:nk, 128:384], zq[h, :, qs]), qb, mask_ref)
+                p = jnp.exp2(st * C2 - lse[h : h + 1, qs])
+                dp = dotf(pj[:nk, 384:640], zdo[h, :, qs])
+                dsv = (p * (dp - d[:, qs])).astype(bf16)
+                pt[:nk, qs] = p.astype(bf16)
+                ds[:nk, qs] = dsv
+                dqt[64 * h : 64 * h + 64, qs] = dotf(pjT[192 + 64 * h : 256 + 64 * h, :nk], dsv).astype(bf16)
+            for k0, k1, q0 in ((0, 512, 0), (512, 768, 512), (768, 1024, 768)):
+                dk = dotf(ds[k0:k1, q0:], qm[q0:, :]).astype(bf16)
+                dv = dotf(pt[k0:k1, q0:], dom[q0:, :]).astype(bf16)
+                dkb[k0:k1] = dk if h == 0 else dkb[k0:k1] + dk
+                dvb[k0:k1] = dv if h == 0 else dvb[k0:k1] + dv
+        point(steps, k, 3)
+        gproj[:, 0:192] = dqt[...].T
+        gproj[:, 192:384] = dkb[:, 0:192]
+        gproj[:, 384:576] = dvb[:, 64:256]
+        vb[0, pl.ds(16 + 2 * t, 1), 0:256] = jnp.sum(gproj[:, 0:256].astype(f32), axis=0, keepdims=True)
+        vb[0, pl.ds(17 + 2 * t, 1), 0:256] = jnp.sum(gproj[:, 384:640].astype(f32), axis=0, keepdims=True)
+        dw = dotf(xT[...], gproj[...])
+        do = dout_b[slot].astype(f32)
+        shape = lambda a: a.astype(bf16).reshape(4, 2, 96, a.shape[1])
+        dwb[k, :, :, :, 0:512] = shape(dw[:, 0:512])
+        dwb[k, :, :, :, 512:640] = shape(dw[:, 512:640] + do[:, 0:128])
+        dwb[k, :, :, :, 640:768] = shape(do[:, 128:256])
+
+        @pl.when(k == 0)
+        def _():
+            q_c0.start()
+
+        @pl.when(k == 1)
+        def _():
+            q_c0.wait_recv()
+            add_into(dwb.at[1], cr.at[0], 8, lambda j: (j // 2, j % 2), lambda j: (j // 2, j % 2))
+            q_y.start()
+
+        @pl.when(k == 2)
+        def _():
+            q_c1.start()
+
+        @pl.when(k == 3)
+        def _():
+            q_c1.wait_recv()
+            add_into(dwb.at[3], cr.at[1], 8, lambda j: (j // 2, j % 2), lambda j: (j // 2, j % 2))
+            q_y.wait_recv()
+            add_into(dwb.at[3], yr, 8, lambda j: (j // 2, j % 2), lambda j: (j // 2, j % 2))
+            for q in q_x:
+                q.start()
+
+        dxa[...] += dot_nt(gproj[...], w[...].reshape(768, 768)[:, 0:640])
+        return 0
+
+    lax.fori_loop(0, 4, group, 0)
+    xst[...] = dxa[...].astype(bf16).reshape(4, 256, 768)
+    v_q = [rcopy(vb.at[0], vr.at[0], sems, pc.peer("c"))]
+    v_q[0].start()
+    xx = exchange(pc, xst, xo_ref, sems)
+    l_o.append(local(xst.at[pc.t], xo_ref.at[pc.t], ls.at[8]))
+
+    def vstep(n, dim):
+        v_q[n].wait_recv()
+        vb[n + 1] = vb[n] + vr[n]
+        v_q.append(rcopy(vb.at[n + 1], vr.at[n + 1], sems, pc.peer(dim)))
+        v_q[n + 1].start()
+
+    vstep(0, "x")
+    red[1].s3()
+    for i in range(2):
+        q_x[i].wait_recv()
+        for z in range(4):
+            dwb[3, z, pc.x, half[i]] = (dwb[3, z, pc.x, half[i]].astype(f32) + xr[i, z].astype(f32)).astype(bf16)
+        for q in q_z[i]:
+            q.start()
+    vstep(1, "y")
+    red[3].s2()
+    red[2].s3()
+    v_q[2].wait_recv()
+    vb[3] = vb[2] + vr[2]
+    v_z = [rcopy(vb.at[3], vr.at[2 + j], sems, pc.peer("z", j)) for j in (3, 2, 1)]
+    for q in v_z:
+        q.start()
+    red[0].s4(gs_ref.at[2], slice(0, 48))
+    red[1].s4(gs_ref.at[2], slice(48, 96))
+    red[3].s3()
+    for i in range(2):
+        for q in q_z[i]:
+            q.wait_recv()
+        gs_ref[0, 48 * i : 48 * i + 48] = (dwb[3, pc.z, pc.x, half[i]].astype(f32) + zr[i, 0].astype(f32)) + (zr[i, 1].astype(f32) + zr[i, 2].astype(f32))
+    red[2].s4(gs_ref.at[1], slice(0, 48))
+    for q in v_z:
+        q.wait_recv()
+    vs_ref[...] = (vb[3] + vr[3]) + (vr[4] + vr[5])
+    red[3].s4(gs_ref.at[1], slice(48, 96))
+    for q in l_o:
+        q.wait()
+    for q in ox + xx:
+        q.wait()
+    for n in range(4):
+        red[n].end()
+    for q in [q_c0, q_y, q_c1] + q_x + q_z[0] + q_z[1] + v_q + v_z:
+        q.wait_send()
+
+
+def back(prefix, x, g1low, g1, g, proj, projT, ot, lse, doutw, d, v, out4):
+    v_ = pltpu.VMEM
+    dma = pltpu.SemaphoreType.DMA
+    sd = jax.ShapeDtypeStruct
+    return pl.pallas_call(
+        back_kernel,
+        out_shape=[sd((3, 96, 768), f32), sd((24, 768), f32), sd((4, 256, 768), bf16), sd((4, 256, 768), bf16)],
+        in_specs=[pl.BlockSpec(memory_space=pltpu.SMEM)] + [HBM] * 10 + [VM, HBM],
+        out_specs=[VM, VM, HBM, HBM],
+        scratch_shapes=[
+            v_((768, L), bf16), v_((L, 768), bf16), v_((L, 768), f32),
+            v_((2, 4, 2, 96, 768), bf16), v_((2, L, 640), bf16), v_((2, 640, L), bf16), v_((2, 256, L), bf16), v_((2, 8, L), f32), v_((2, 768, 256), bf16),
+            v_((3, 256, L), bf16), v_((3, 256, L), bf16), v_((L, 256), bf16), v_((L, 256), bf16), v_((L, L), bf16), v_((L, L), bf16),
+            v_((4, 256, 256), f32), v_((256, L), bf16), v_((192, L), bf16), v_((L, 256), bf16), v_((L, 256), bf16), v_((L, 640), bf16),
+            v_((4, 2, 4, 2, 48, 768), bf16), v_((4, 2, 4, 2, 48, 768), bf16), v_((4, 2, 4, 48, 768), bf16), v_((4, 3, 2, 48, 768), bf16), v_((4, 48, 768), bf16),
+            v_((4, 4, 2, 96, 768), bf16), v_((2, 4, 2, 96, 768), bf16), v_((4, 2, 96, 768), bf16), v_((2, 4, 48, 768), bf16), v_((2, 3, 48, 768), bf16),
+            v_((4, 24, 768), f32), v_((6, 24, 768), f32), v_((4, 256, 768), bf16),
+            dma((N_C,)), dma((N_C,)), dma((9,)), dma((2, 6)),
+        ],
+        compiler_params=pltpu.CompilerParams(collective_id=1, has_side_effects=True, vmem_limit_bytes=67043328),
+    )(prefix, x, g1low, g1, g, proj, projT, ot, lse, doutw, d, v, out4)
 
 
 EPSILON = 1e-12
@@ -312,7 +495,7 @@
     gn = g2 + ein("tpf,tdf->pd", gpre, w2)
     g1, dgain1, dshift1 = norm_back(gn, gain1, xhat1, inv1)
     g1low = g1.astype(bf16)
-    dout = ein("pd,tpw->tdw", g1low, heads[:, :, 64:]).astype(bf16)
+    dout = ein("pd,tpw->tdw", g1low, heads).astype(bf16)
     dbh = jnp.sum(gpre, 1, dtype=f32)
     return out, g1, g1low, dout, d2, d3, (dgain1, dgain2, dshift1, dshift2, jnp.sum(g1, 0), dbh, jnp.sum(g2, 0))
 
@@ -342,27 +525,33 @@
     bqkv = jnp.pad(jnp.stack([vec[0].reshape(4, 192), jnp.zeros((4, 192), f32), vec[1].reshape(4, 192)], 1).reshape(4, 1, 576), ((0, 0), (0, 0), (0, 64)))
     my_prefix = lax.dynamic_slice_in_dim(prefix, t_me, 1, 0)
     proj, projT, heads, ot, lse = attn_fwd(my_prefix, x, w1, bqkv)
-    out, g1, g1low, dout, d2, d3, small = middle(
+    out, g1, g1low, doutw, d2, d3, small = middle(
         x, cs.reshape(1024, 768), heads, w1, w2, w3, vec[2], vec[3:7].reshape(4, 768), vec[7], vec[8], vec[9], vec[10], vec[11]
     )
-    gproj = attn_bwd(my_prefix, g1low, w1, proj, projT, ot, lse)
     ein = functools.partial(jnp.einsum, preferred_element_type=f32)
-    gp = gproj[:, :, :576]
-    dqkv = ein("pd,tpc->tdc", x, gp).astype(bf16)
-    dx = (g1 + ein("tpc,tdc->pd", gp, w1[:, :, :576])).astype(bf16)
     dgain1, dgain2, dshift1, dshift2, dbo, dbh, dbd = small
-    dbq = jnp.sum(gp[:, :, :192], 1, dtype=f32).reshape(768)
-    dbv = jnp.sum(gp[:, :, 384:], 1, dtype=f32).reshape(768)
-    v = jnp.concatenate([jnp.stack([dbq, dbv, dbo]), dbh, jnp.stack([dbd, dshift1, dshift2, dgain1, dgain2]), jnp.zeros((4, 768), f32)])
-    d = jnp.stack([jnp.concatenate([dqkv, dout], 2), d2, d3])
-    o4, x4 = out.reshape(4, 256, 768), dx.reshape(4, 256, 768)
+    o4 = out.reshape(4, 256, 768)
+    none = jnp.zeros((1, 768), f32)
+    v = [none, none, dbo[None], dbh, jnp.stack([dbd, dshift1, dshift2, dgain1, dgain2]), jnp.zeros((4, 768), f32)]
     if lax.axis_size("dp") == 8:
-        gs, vs, oo, xx = reduce_all(d.reshape(3, 2, 2, 4, 2, rows, 768), v, o4, x4)
+        gs, vs, oo, xx = back(
+            my_prefix, xs, g1low, g1, g, proj, projT, ot, lse, doutw, jnp.stack([d2, d3]).reshape(2, 2, 2, 4, 2, rows, 768),
+            jnp.concatenate(v + [jnp.zeros((8, 768), f32)]), o4,
+        )
+        qv = vs[16:24, :256].reshape(4, 2, 256)
+        vs = jnp.concatenate([qv[:, 0, :192].reshape(1, 768), qv[:, 1, :192].reshape(1, 768), vs[2:16]])
     else:
+        gproj = attn_bwd(my_prefix, g1low, w1, proj, projT, ot, lse)
+        gp = gproj[:, :, :576]
+        dqkv = ein("pd,tpc->tdc", x, gp).astype(bf16)
+        x4 = (g1 + ein("tpc,tdc->pd", gp, w1[:, :, :576])).astype(bf16).reshape(4, 256, 768)
+        v[0] = jnp.sum(gp[:, :, :192], 1, dtype=f32).reshape(1, 768)
+        v[1] = jnp.sum(gp[:, :, 384:], 1, dtype=f32).reshape(1, 768)
+        d = jnp.stack([jnp.concatenate([dqkv, doutw[:, :, 64:]], 2), d2, d3])
         part = lax.all_to_all(d, "tensor", 1, 1, tiled=True).astype(f32).sum(1)
         part = part.astype(bf16).reshape(3, -1, rows, 768)
         gs = lax.all_to_all(part, "dp", 1, 1, tiled=True).astype(f32).sum(1)
-        vs = lax.psum(v, ("dp", "tensor"))
+        vs = lax.psum(jnp.concatenate(v), ("dp", "tensor"))
         oo = lax.all_to_all(o4, "tensor", 0, 0, tiled=True)
         xx = lax.all_to_all(x4, "tensor", 0, 0, tiled=True)
     mine = lax.dynamic_slice_in_dim(vs, (d_me * n_t + t_me) * width, width, 1)

time: 536 us -> 449 us (0.84)
  Pallas kernels: 338 us -> 279 us
  matrix products: 117 us -> 105 us
  local copies, waits for them, and re-layouts: 45.9 us -> 35.9 us
    pallas_call x2 -> x1, Pallas kernels: 166 us -> 107 us  [back(): pl.pallas_call(back_kernel, out_shape=[sd((3, 96, 768), f32), sd((24, 768...]
    dot_general x3 -> x1, matrix products: 20 us -> 3.08 us  [middle(): dout = ein('pd,tpw->tdw', g1low, heads).astype(bf16)]
    concatenate x2, local copies, waits for them, and re-layouts: 8.09 us -> 2.15 us  [on_device(): jnp.concatenate(v + [jnp.zeros((8, 768), f32)])]
    unnamed x43 -> x41, local copies, waits for them, and re-layouts: 14.5 us -> 10.9 us
where the time goes in v2:
time: 449 us; the launch traced here: 441 us
  Pallas kernels  279 us (62%)
  matrix products  105 us (23%)
  local copies, waits for them, and re-layouts  35.9 us (8%)
  other arithmetic  19.7 us (4%)
    pallas_call x1, Pallas kernels, gather_all(): pl.pallas_call(ag_kernel, out_shape=[jax.ShapeDtypeStruct((3, 2, 2, 4, 2)...  140 us
    pallas_call x1, Pallas kernels, back(): pl.pallas_call(back_kernel, out_shape=[sd((3, 96, 768), f32), sd((24, 768...  107 us
    dot_general x1, matrix products, middle(): pre = ein('pd,tdf->tpf', low, w2) + bias_h[:, None, :]  38.3 us
    pallas_call x1, Pallas kernels, attn_fwd(): pl.pallas_call(fwd_kernel, grid_spec=pltpu.PrefetchScalarGridSpec(num_sca...  31.8 us
    dot_general x1, matrix products, middle(): gpre = gelu_back(ein('pd,tdf->tpf', g2low, w3))[0].astype(bf16)  18.3 us
    another operation x1, local copies, waits for them, and re-layouts, on_device(): w1, w2, w3 = [a.reshape(n_t, 768, 768) for a in g]  11.6 us
    unnamed x41, local copies, waits for them, and re-layouts  10.9 us
    dot_general x1, matrix products, middle(): gn = g2 + ein('tpf,tdf->pd', gpre, w2)  10.5 us

profile of v2, /device:TPU:0, one launch (start us, length us, event | category | flops | bytes accessed | tf_op | source)
XLA Modules:
  0.0 440.8 jit_solution(9500770845492365662)
XLA Ops:
  0.6 0.0 copy-start.10
  0.6 0.0 copy-start.11
  0.7 4.0 copy_bitcast_fusion
  4.7 0.2 copy.37
  4.9 0.2 copy.39
  5.1 0.1 copy.38
  5.2 0.1 maximum_bitcast_fusion
  5.3 0.0 copy-done.9
  5.3 0.0 copy-done.8
  5.3 0.8 pad_maximum_fusion.1.s_ref
  6.1 0.6 select_maximum_fusion.b_ref
  6.7 139.9 %shard_map.152 = (bf16[3,2,2,4,2,96,768]{6,5,4,3,2,1,0:T(8,128)(2,1)}, bf16[4,256,768]{2,1,0:T(8,128)(2,1)}, bf16[4,256,768]{2,1,0:T(8,128)(2,1)}, f32[2,2,4,2,16,128]{5,4,3,2,1,0:T(8,128)}) custom-call(bf16[3,96,768]{2,1,0:T(8,128)(2,1)} %pad_maximum_fusion.1.s_ref, bf16[4,256,768]{2,1,0:T(8,128)(2,1)} %get-tuple-element.89.h_ref, ...), custom_call_target="tpu_custom_call" | custom-call | tf_op jit(solution)/shard_map/pallas_call | solution.py:188
  146.6 1.0 copy.42
  147.6 0.4 slice_reduce_fusion
  148.0 0.1 stack_reshape_squeeze.6
  148.0 0.1 stack_reshape_squeeze.7
  148.1 0.1 pad.16.clone
  148.2 0.1 pad_maximum_fusion.2
  148.3 0.1 reshape.128
  148.4 0.6 pad.9.b_ref
  149.0 0.6 dynamic_slice.6.prefix_ref
  149.6 11.6 %fusion.51 = (bf16[1,2,2,4,2,96,768]{6,5,4,3,2,1,0:T(8,128)(2,1)}, bf16[1,2,2,4,2,96,768]{6,5,4,3,2,1,0:T(8,128)(2,1)}, bf16[1,2,2,4,2,96,768]{6,5,4,3,2,1,0:T(8,128)(2,1)}) fusion(bf16[3,2,2,4,2,96,768]{6,5,4,3,2,1,0:T(8,128)(2,1)} %get-tuple-element.24.w_ref), kind=kLoop, calls=%fused_computation.109 | loop fusion | bytes 28311552 | tf_op jit(solution)/shard_map/unstack | solution.py:522
  161.2 31.8 %shard_map.153 = (bf16[4,1024,640]{2,1,0:T(8,128)(2,1)}, bf16[4,640,1024]{2,1,0:T(8,128)(2,1)}, bf16[4,1024,256]{2,1,0:T(8,128)(2,1)}, bf16[4,256,1024]{2,1,0:T(8,128)(2,1)}, f32[4,8,1024]{2,1,0:T(8,128)}) custom-call(s32[1]{0:T(128)} %dynamic_slice.6.prefix_ref, bf16[1024,768]{1,0:T(8,128)(2,1)} %bitcast.185, bf16[4,768,768]{2,1,0:T(8,128)(2,1)} %bitcast.183, ...), custom_call_target="tpu_custom_call" | custom-call | tf_op jit(solution)/shard_map/pallas_call | solution.py:55
  193.0 0.1 add.91
  193.1 4.5 %fusion.52 = (f32[1024]{0:T(1024)S(1)}, f32[1024,768]{1,0:T(8,128)S(1)}) fusion(f32[768]{0:T(1024)S(1)} %add.91, bf16[4,1024,256]{2,1,0:T(8,128)(2,1)} %get-tuple-element.25, bf16[4,768,768]{2,1,0:T(8,128)(2,1)} %bitcast.184, bf16[1024,768]{1,0:T(8,128)(2,1)} %bitcast.186), kind=kOutput, calls=%fused_computation.110 | convolution fusion | flops 1613757440 | bytes 8395776 | tf_op jit(solution)/shard_map/tpw,tdw->pd/dot_general | solution.py:480
  197.6 0.5 multiply_reduce_fusion.3
  198.1 0.1 mul.149
  198.2 0.1 add.95
  198.3 0.1 add.98
  198.4 38.3 %fusion.9 = (bf16[4,1024,768]{1,2,0:T(8,128)(2,1)}, f32[4,1024,768]{1,2,0:T(8,128)}, f32[4,768,1024]{2,1,0:T(8,128)}) fusion(f32[4,768]{1,0:T(4,128)S(1)} %add.98, bf16[4,768,768]{2,1,0:T(8,128)(2,1)} %bitcast.188, f32[1024,768]{1,0:T(8,128)S(1)} %get-tuple-element.81, f32[768]{0:T(1024)S(1)} %add.95, f32[768]{0:T(1024)S(1)} %mul.149, ...), kind=kOutput, calls=%fused_computation.17 | convolution fusion | flops 5043388416 | bytes 39348224 | tf_op jit(solution)/shard_map/pd,tdf->tpf/dot_general | solution.py:484
  236.7 0.0 copy-done.2
  236.7 0.1 add.102
  236.8 10.1 %fusion.53 = (f32[1024]{0:T(1024)S(1)}, f32[1024,768]{1,0:T(8,128)S(1)}) fusion(f32[768]{0:T(1024)S(1)} %add.102, bf16[4,1024,768]{1,2,0:T(8,128)(2,1)} %get-tuple-element.72, bf16[4,768,768]{2,1,0:T(8,128)(2,1)} %bitcast.190, f32[768]{0:T(1024)S(1)} %add.95, f32[768]{0:T(1024)S(1)} %mul.149, f32[1024]{0:T(1024)S(1)} %add_rsqrt_fusion.1, ...), kind=kOutput, calls=%fused_computation.111 | convolution fusion | flops 4837342208 | bytes 17323008 | tf_op jit(solution)/shard_map/tpf,tdf->pd/dot_general | solution.py:487
  246.9 0.5 multiply_reduce_fusion.2
  247.4 0.1 mul.141
  247.5 0.1 add.107
  247.6 3.9 fusion.30
  251.6 0.8 convert_reduce_fusion.1
  252.3 2.4 fusion.47
  254.7 18.3 %convert_reduce_fusion = (f32[4,768]{1,0:T(4,128)S(1)}, bf16[4,1024,768]{1,2,0:T(8,128)(2,1)}) fusion(f32[4,1024,768]{1,2,0:T(8,128)} %get-tuple-element.73, bf16[4,768,768]{2,1,0:T(8,128)(2,1)} %bitcast.191, f32[1024,768]{1,0:T(8,128)} %get-tuple-element.69, f32[4,768,1024]{2,1,0:T(8,128)} %get-tuple-element.82, f32[4,768]{1,0:T(4,128)S(1)} %add.98), kind=kOutput, calls=%fused_computation.18 | convolution fusion | flops 4886098944 | bytes 39346176 | tf_op jit(solution)/shard_map/pd,tdf->tpf/dot_general | solution.py:493
  273.1 0.0 copy-done.3
  273.1 10.5 %multiply_reduce_fusion = (f32[768]{0:T(1024)S(1)}, f32[1024]{0:T(1024)S(1)}, f32[1024]{0:T(1024)S(1)}, f32[768]{0:T(1024)S(1)}, f32[1024,768]{1,0:T(8,128)S(1)}) fusion(f32[1024,768]{1,0:T(8,128)S(1)} %copy-done.3, f32[1024]{0:T(1024)S(1)} %add_rsqrt_fusion.1, f32[1024]{0:T(1024)S(1)} %broadcast_multiply_fusion.4, f32[768]{0:T(1024)S(1)} %mul.149, ...), kind=kOutput, calls=%fused_computation.50 | convolution fusion | flops 4839698432 | bytes 20472832 | tf_op jit(solution)/shard_map/tpf,tdf->pd/dot_general | solution.py:495
  283.7 1.6 fusion.49
  285.4 2.1 concatenate.19.v_ref
  287.6 10.5 %convolution_convert_fusion.1 = bf16[4,768,768]{1,2,0:T(8,128)(2,1)} fusion(bf16[4,1024,768]{1,2,0:T(8,128)(2,1)} %get-tuple-element.87, f32[1024,768]{1,0:T(8,128)} %copy-done.2, f32[768]{0:T(1024)S(1)} %add.95, f32[768]{0:T(1024)S(1)} %mul.149, f32[1024]{0:T(1024)S(1)} %add_rsqrt_fusion.1, f32[1024]{0:T(1024)S(1)} %broadcast_multiply_fusion.4), kind=kOutput, calls=%fused_computation.59 | convolution fusion | flops 4838129664 | bytes 14170112 | tf_op jit(solution)/shard_map/pd,tpf->tdf/dot_general | solution.py:494
  298.0 9.5 %convolution_convert_fusion = bf16[4,768,768]{1,2,0:T(8,128)(2,1)} fusion(bf16[4,1024,768]{1,2,0:T(8,128)(2,1)} %get-tuple-element.72, f32[1024,768]{1,0:T(8,128)S(1)} %copy-done.6), kind=kOutput, calls=%fused_computation.58 | convolution fusion | flops 4834983936 | bytes 14155776 | tf_op jit(solution)/shard_map/pd,tpf->tdf/dot_general | solution.py:492
  307.6 8.2 %pad_maximum_fusion.d_ref = bf16[2,2,2,4,2,96,768]{6,5,4,3,2,1,0:T(8,128)(2,1)} fusion(bf16[1,2,2,4,2,96,768]{6,5,4,3,2,1,0:T(8,128)(2,1)} %bitcast.193, bf16[1,2,2,4,2,96,768]{6,5,4,3,2,1,0:T(8,128)(2,1)} %bitcast.192), kind=kLoop, calls=%fused_computation.32 | loop fusion | flops 4718592 | bytes 18874368 | tf_op jit(solution)/shard_map/stack | solution.py:538
  315.8 0.2 convert_element_type.63.g_ref
  315.9 1.4 copy-done.15
  317.4 3.1 fusion.37.dout_ref
  320.4 107.3 %shard_map.154 = (f32[3,96,768]{2,1,0:T(8,128)}, f32[24,768]{1,0:T(8,128)}, bf16[4,256,768]{2,1,0:T(8,128)(2,1)}, bf16[4,256,768]{2,1,0:T(8,128)(2,1)}) custom-call(s32[1]{0:T(128)} %dynamic_slice.6.prefix_ref, bf16[4,256,768]{2,1,0:T(8,128)(2,1)} %get-tuple-element.21.x_ref, bf16[1024,768]{1,0:T(8,128)(2,1)} %copy-done.5, f32[1024,768]{1,0:T(8,128)} %copy-done, ...), custom_call_target="tpu_custom_call" | custom-call | tf_op jit(solution)/shard_map/pallas_call | solution.py:443
  427.7 1.0 slice.90
  428.7 0.7 slice.87
  429.4 0.1 reshape_squeeze.10
  429.5 0.1 reshape_squeeze.11
  429.6 0.1 fusion.43
  429.7 0.6 slice.107
  430.3 3.8 copy.59
  434.0 3.8 copy.60
  437.8 0.1 copy.56
  438.0 0.9 copy.61
  438.8 0.8 slice_bitcast_fusion
  439.7 0.1 slice_bitcast_fusion.3
  439.8 0.7 copy.62
  (52 shorter events, 0.2 us)
Async XLA Ops:
  0.6 4.1 copy-start.10
  0.6 4.4 %copy-start.11 = (bf16[192,96]{1,0:T(8,128)(2,1)S(1)}, bf16[192,96]{1,0:T(8,128)(2,1)}, u32[]{:S(2)}) copy-start(bf16[192,96]{1,0:T(8,128)(2,1)} %param.13) | copy-start | bytes 110596
  0.7 4.6 %copy-start.9 = (bf16[96,768]{1,0:T(8,128)(2,1)S(1)}, bf16[96,768]{1,0:T(8,128)(2,1)}, u32[]{:S(2)}) copy-start(bf16[96,768]{1,0:T(8,128)(2,1)} %param.14) | copy-start | bytes 442372
  0.7 4.6 %copy-start.8 = (bf16[768,96]{0,1:T(8,128)(2,1)S(1)}, bf16[768,96]{0,1:T(8,128)(2,1)}, u32[]{:S(2)}) copy-start(bf16[768,96]{0,1:T(8,128)(2,1)} %param.15) | copy-start | bytes 442372
  0.7 5.4 %copy-start.13 = (f32[10,24]{1,0:T(8,128)S(1)}, f32[10,24]{1,0:T(8,128)}, u32[]{:S(2)}) copy-start(f32[10,24]{1,0:T(8,128)} %param.16) | copy-start | bytes 2884
  0.7 5.4 %copy-start.14 = (f32[2,24]{1,0:T(2,128)S(1)}, f32[2,24]{1,0:T(2,128)}, u32[]{:S(2)}) copy-start(f32[2,24]{1,0:T(2,128)} %param.17) | copy-start | bytes 580
  4.7 144.2 %copy-start.16 = (s32[4]{0:T(128)S(1)}, s32[4]{0:T(128)}, u32[]{:S(2)}) copy-start(s32[4]{0:T(128)} %param.11) | copy-start | bytes 52
  197.6 39.2 %copy-start.2 = (f32[1024,768]{1,0:T(8,128)}, f32[1024,768]{1,0:T(8,128)S(1)}, u32[]{:S(2)}) copy-start(f32[1024,768]{1,0:T(8,128)S(1)} %get-tuple-element.81) | copy-start | bytes 9437188
  247.6 3.9 copy-start.1
  254.7 18.3 %copy-start.3 = (f32[1024,768]{1,0:T(8,128)S(1)}, f32[1024,768]{1,0:T(8,128)}, u32[]{:S(2)}) copy-start(f32[1024,768]{1,0:T(8,128)} %copy-done.2) | copy-start | bytes 9437188
  273.1 10.6 %copy-start.4 = (f32[1024,768]{1,0:T(8,128)S(1)}, f32[1024,768]{1,0:T(8,128)}, u32[]{:S(2)}) copy-start(f32[1024,768]{1,0:T(8,128)} %copy-done.2) | copy-start | bytes 9437188
  285.3 30.5 %copy-start = (f32[1024,768]{1,0:T(8,128)}, f32[1024,768]{1,0:T(8,128)S(1)}, u32[]{:S(2)}) copy-start(f32[1024,768]{1,0:T(8,128)S(1)} %get-tuple-element.71.gf_ref) | copy-start | bytes 9437188
  287.6 10.5 %copy-start.6 = (f32[1024,768]{1,0:T(8,128)S(1)}, f32[1024,768]{1,0:T(8,128)}, u32[]{:S(2)}) copy-start(f32[1024,768]{1,0:T(8,128)} %get-tuple-element.69) | copy-start | bytes 9437188
  315.8 1.6 copy-start.15
  317.4 3.1 copy-start.5
  427.7 10.1 %copy-start.7 = (f32[3,96,768]{2,1,0:T(8,128)S(1)}, f32[3,96,768]{2,1,0:T(8,128)}, u32[]{:S(2)}) copy-start(f32[3,96,768]{2,1,0:T(8,128)} %get-tuple-element.32) | copy-start | bytes 2654212
  429.7 10.8 %copy-start.12 = (f32[16,24]{1,0:T(8,128)}, f32[16,24]{1,0:T(8,128)S(1)}, u32[]{:S(2)}) copy-start(f32[16,24]{1,0:T(8,128)S(1)} %fusion.43) | copy-start | bytes 4612
